TPU v7x, 128 devices: a whole 4x4x4 slice. The times are simulated.
128 devices in a mesh: ra: 16 (over x, y_hi, core), dec: 8 (over z, y_lo).
Axes of the slice: x: 4, y: 4 (y_hi: 2, y_lo: 2; y = y_hi * 2 + y_lo), z: 4, core: 2. Of those that a mesh axis runs over, the one named last changes fastest.
Arguments:
- log_flux: float32 [5, 32768], P(None, ('ra', 'dec')), may hold values from 5.5 to 9.5
- position: float32 [2, 32768], P(None, ('ra', 'dec')), may hold values from 0 to 640
- log_width: float32 [32768], P(('ra', 'dec')), may hold values from -3.5 to -0.5
- owner_tile: int32 [32768, 1], P(('ra', 'dec')), may hold values from 0 to 127; in each aligned block of 256 rows (0 to 255, 256 to 511, ...) at most 4 rows name the same one
- sky_level: float32 [16, 8, 5], P('ra', 'dec'), may hold values from 0.5 to 4
- counts: int32 [5, 10240, 5120], P(None, 'ra', 'dec'), may hold values from 0 to 7
Outputs:
- gradient: float32 [8, 32768], P(None, ('ra', 'dec'))
Inputs may be any that keep to these rules, and one draw needn't show every extreme that they name: `owner_tile`: in each aligned block of 256 catalog rows (the rows of one device) no tile is named more than 4 times, a bound that some block reaches.
All inputs are finite; a program needn't handle non-finite values.
Results may differ from a plain program's by a relative error of at most 0.00095.
Values may be sent and summed in bfloat16 or wider, within the bound.
A program may use at most 128 MiB of HBM per device.

v0:
```python
import math

import jax
import jax.numpy as jnp
from jax import lax
from jax.sharding import PartitionSpec as P

MARGIN = 128
CAT_DEV = 256


def passed_along(value, axis, steps):
    count = lax.axis_size(axis)
    leading, last = (max(0, -steps), min(count, count - steps))
    return lax.ppermute(value, axis, [(source, source + steps) for source in range(leading, last)])


def with_halo(cells, sides, width):
    for axis, dim in sides:
        count = lax.axis_size(axis)
        ends = count - 1
        head = lax.slice_in_dim(cells, 0, width, axis=dim)
        tail = lax.slice_in_dim(cells, cells.shape[dim] - width, cells.shape[dim], axis=dim)
        cells = jnp.concatenate(
            [
                lax.ppermute(tail, axis, [(i, (i + 1) % count) for i in range(ends)]),
                cells,
                lax.ppermute(head, axis, [((i + 1) % count, i) for i in range(ends)]),
            ],
            axis=dim,
        )
    return cells


def profiles(center, log_width, length):
    coords = jnp.arange(length, dtype=jnp.float32) - MARGIN + 0.5
    sigma = MARGIN * jnp.exp(log_width)
    offset = (coords[:, None] - center[None, :]) / sigma[None, :]
    shape = jnp.exp(-0.5 * offset * offset) / (math.sqrt(2.0 * math.pi) * sigma[None, :])
    return (shape, offset, sigma)


def on_device(log_flux, position, log_width, owner_tile, sky_level, counts):
    tile_count = lax.axis_size("ra") * lax.axis_size("dec")
    capacity = max(2, 2 * CAT_DEV // tile_count)
    slot_count = tile_count * capacity
    tile_side = counts.shape[1]
    canvas_side = tile_side + 2 * MARGIN
    rows_here = log_flux.shape[1]
    target_tile = owner_tile[:, 0]
    order = jnp.arange(rows_here, dtype=jnp.int32)
    matches = (target_tile[:, None] == target_tile[None, :]) & (order[None, :] < order[:, None])
    rank_in = jnp.sum(matches.astype(jnp.int32), axis=1)
    target_slot = target_tile * capacity + rank_in
    onehot = (target_slot[:, None] == jnp.arange(slot_count, dtype=jnp.int32)[None, :]).astype(
        jnp.float32
    )
    params = jnp.concatenate(
        [log_flux, position, log_width[None, :], jnp.ones((1, rows_here), jnp.float32)], axis=0
    )
    outgoing = jnp.dot(params, onehot, precision=lax.Precision.HIGHEST)
    arrived = lax.all_to_all(outgoing, ("ra", "dec"), split_axis=1, concat_axis=1, tiled=True)
    flux_values = arrived[8][None, :] * jnp.exp(arrived[0:5])
    row_prof, row_off, sigma = profiles(arrived[5], arrived[7], canvas_side)
    col_prof, col_off, _ = profiles(arrived[6], arrived[7], canvas_side)
    row_bf = row_prof.astype(jnp.bfloat16)
    col_bf = col_prof.astype(jnp.bfloat16)
    scaled = (row_prof[None, :, :] * flux_values[:, None, :]).astype(jnp.bfloat16)
    canvas = jnp.einsum("bis,js->bij", scaled, col_bf, preferred_element_type=jnp.float32).astype(
        jnp.bfloat16
    )
    edge = MARGIN
    inner_end = edge + tile_side
    rim_start = tile_side - edge
    interior = canvas[:, edge:inner_end, edge:inner_end].astype(jnp.float32)
    from_below = passed_along(canvas[:, :edge, edge:inner_end], "ra", -1)
    from_above = passed_along(canvas[:, inner_end:, edge:inner_end], "ra", 1)
    from_right = passed_along(canvas[:, edge:inner_end, :edge], "dec", -1)
    from_left = passed_along(canvas[:, edge:inner_end, inner_end:], "dec", 1)
    interior = interior.at[:, rim_start:, :].add(from_below.astype(jnp.float32))
    interior = interior.at[:, :edge, :].add(from_above.astype(jnp.float32))
    interior = interior.at[:, :, rim_start:].add(from_right.astype(jnp.float32))
    interior = interior.at[:, :, :edge].add(from_left.astype(jnp.float32))
    upper_pair = jnp.concatenate([canvas[:, :edge, :edge], canvas[:, :edge, inner_end:]], axis=2)
    lower_pair = jnp.concatenate(
        [canvas[:, inner_end:, :edge], canvas[:, inner_end:, inner_end:]], axis=2
    )
    below_pair = passed_along(upper_pair, "ra", -1)
    above_pair = passed_along(lower_pair, "ra", 1)
    leftward = jnp.concatenate([below_pair[:, :, :edge], above_pair[:, :, :edge]], axis=1)
    rightward = jnp.concatenate([below_pair[:, :, edge:], above_pair[:, :, edge:]], axis=1)
    got_left = passed_along(leftward, "dec", -1).astype(jnp.float32)
    got_right = passed_along(rightward, "dec", 1).astype(jnp.float32)
    interior = interior.at[:, rim_start:, rim_start:].add(got_left[:, :edge])
    interior = interior.at[:, :edge, rim_start:].add(got_left[:, edge:])
    interior = interior.at[:, rim_start:, :edge].add(got_right[:, :edge])
    interior = interior.at[:, :edge, :edge].add(got_right[:, edge:])
    intensity = sky_level.reshape(-1)[:, None, None] + interior
    weights = (counts.astype(jnp.float32) / intensity - 1.0).astype(jnp.bfloat16)
    weight_canvas = with_halo(weights, (("ra", 1), ("dec", 2)), MARGIN)
    along_rows = jnp.einsum(
        "bij,js->bis", weight_canvas, col_bf, preferred_element_type=jnp.float32
    )
    along_cols = jnp.einsum(
        "bij,is->bjs", weight_canvas, row_bf, preferred_element_type=jnp.float32
    )
    flux_grad = flux_values * jnp.sum(row_bf.astype(jnp.float32)[None, :, :] * along_rows, axis=1)
    row_total = jnp.sum(flux_values[:, None, :] * along_rows, axis=0)
    col_total = jnp.sum(flux_values[:, None, :] * along_cols, axis=0)
    row_grad = jnp.sum(row_prof * row_off / sigma[None, :] * row_total, axis=0)
    col_grad = jnp.sum(col_prof * col_off / sigma[None, :] * col_total, axis=0)
    width_grad = jnp.sum(row_prof * (row_off * row_off - 1.0) * row_total, axis=0) + jnp.sum(
        col_prof * (col_off * col_off - 1.0) * col_total, axis=0
    )
    slot_grad = jnp.concatenate(
        [flux_grad, row_grad[None], col_grad[None], width_grad[None]], axis=0
    )
    returned = lax.all_to_all(slot_grad, ("ra", "dec"), split_axis=1, concat_axis=1, tiled=True)
    return jnp.dot(returned, onehot.T, precision=lax.Precision.HIGHEST)


def solution(mesh):
    in_specs = (
        P(None, ("ra", "dec")),
        P(None, ("ra", "dec")),
        P(("ra", "dec")),
        P(("ra", "dec"), None),
        P("ra", "dec", None),
        P(None, "ra", "dec"),
    )
    out_specs = P(None, ("ra", "dec"))
    return jax.shard_map(
        on_device, mesh=mesh, in_specs=in_specs, out_specs=out_specs, check_vma=False
    )
```

profile of v0, /device:TPU:1, one launch (start us, length us, event | category | flops | bytes accessed | tf_op | source)
XLA Modules:
  0.0 254.1 jit_solution(15445283636594914386)
XLA Ops:
  0.0 0.9 convert_reduce_fusion
  0.9 0.7 multiply_add_fusion
  1.7 2.1 fusion.21
  3.8 11.5 %all-to-all-start = ((f32[9,128,4]{0,2,1:T(4,128)}), f32[9,128,4]{0,2,1:T(4,128)S(1)}, u32[]{:S(2)}, u32[]{:S(2)}) async-start(f32[9,128,4]{0,2,1:T(4,128)} %bitcast.4), calls=%async_computation | async-start | bytes 524288 | tf_op jit(solution)/shard_map/all_to_all | solution.py:62
  15.4 0.6 fusion.45
  15.9 1.4 and_reduce_fusion
  17.4 10.3 %copy.91 = s32[5,640,640]{1,2,0:T(8,128)} copy(s32[5,640,640]{2,1,0:T(8,128)} %param.27) | data formatting | bytes 16384000 | tf_op args[5]
  27.6 0.1 copy.101
  27.8 0.2 copy.92
  27.9 0.2 exp.35
  28.2 1.3 slice_reduce_fusion.1
  29.5 0.1 sub.50
  29.6 0.1 mul.154
  29.7 0.1 mul.149
  29.8 0.1 sub.53
  29.9 0.1 mul.157
  30.0 0.5 fusion.17
  30.5 5.1 %convolution_convert_fusion = bf16[5,896,896]{1,2,0:T(8,128)(2,1)S(1)} fusion(f32[5,512]{1,0:T(8,128)S(1)} %broadcast_multiply_fusion, f32[896,512]{1,0:T(8,128)S(1)} %get-tuple-element.132, f32[512]{0:T(512)S(1)} %mul.154, f32[512]{0:T(512)S(1)} %mul.149, f32[512]{0:T(512)S(1)} %sub.53, f32[896]{0:T(1024)S(1)} %iota_add_fusion), kind=kOutput, calls=%fused_computation.6 | convolution fusion | flops 4121772032 | bytes 9883136 | tf_op jit(solution)/shard_map/bis,js->bij/dot_general | solution.py:69
  35.6 0.1 fusion.39
  35.8 0.3 fusion.41
  36.1 5.1 %collective-permute-start.5 = (bf16[5,128,256]{1,2,0:T(8,128)(2,1)S(1)}, bf16[5,128,256]{1,2,0:T(8,128)(2,1)S(1)}, u32[]{:S(2)}, u32[]{:S(2)}) collective-permute-start(bf16[5,128,256]{1,2,0:T(8,128)(2,1)S(1)} %pad_maximum_fusion.5), channel_id=1, source_target_pairs={{0,8},{8,16},{16,24},{24,32},{32,40},{40,48},{48,56},{56,64},{64,7... | collective-permute-start | bytes 983048 | tf_op jit(solution)/shard_map/ppermute | solution.py:15
  41.2 1.9 collective-permute-start.4
  43.2 0.2 fusion.40
  43.3 5.1 %collective-permute-start.1 = (bf16[5,128,640]{1,2,0:T(8,128)(2,1)S(1)}, bf16[5,128,640]{1,2,0:T(8,128)(2,1)S(1)}, u32[]{:S(2)}, u32[]{:S(2)}) collective-permute-start(bf16[5,128,640]{1,2,0:T(8,128)(2,1)S(1)} %get-tuple-element.120), channel_id=1, source_target_pairs={{0,8},{8,16},{16,24},{24,32},{32,40},{40,48},{48,56},{56,64},{64,7... | collective-permute-start | bytes 2457608 | tf_op jit(solution)/shard_map/ppermute | solution.py:15
  48.5 1.9 collective-permute-start
  50.4 1.3 collective-permute-start.2
  51.9 1.3 collective-permute-start.6
  53.2 4.6 %collective-permute-start.7 = (bf16[5,256,128]{1,2,0:T(8,128)(2,1)S(1)}, bf16[5,256,128]{1,2,0:T(8,128)(2,1)S(1)}, u32[]{:S(2)}, u32[]{:S(2)}) collective-permute-start(bf16[5,256,128]{1,2,0:T(8,128)(2,1)S(1)} %pad_maximum_fusion.7), channel_id=1, source_target_pairs={{0,1},{1,2},{2,3},{3,4},{4,5},{5,6},{6,7},{8,9},{9,10},{10,11},{11... | collective-permute-start | bytes 983048 | tf_op jit(solution)/shard_map/ppermute | solution.py:15
  57.8 0.6 slice_convert_fusion
  58.4 43.4 %collective-permute-done.6 = bf16[5,256,128]{1,2,0:T(8,128)(2,1)S(1)} collective-permute-done((bf16[5,256,128]{1,2,0:T(8,128)(2,1)S(1)}, bf16[5,256,128]{1,2,0:T(8,128)(2,1)S(1)}, u32[]{:S(2)}, u32[]{:S(2)}) %collective-permute-start.6) | collective-permute-done | bytes 327712 | tf_op jit(solution)/shard_map/ppermute | solution.py:15
  101.8 3.6 %collective-permute-start.3 = (bf16[5,640,128]{1,2,0:T(8,128)(2,1)S(1)}, bf16[5,640,128]{1,2,0:T(8,128)(2,1)S(1)}, u32[]{:S(2)}, u32[]{:S(2)}) collective-permute-start(bf16[5,640,128]{1,2,0:T(8,128)(2,1)S(1)} %get-tuple-element.118), channel_id=1, source_target_pairs={{0,1},{1,2},{2,3},{3,4},{4,5},{5,6},{6,7},{8,9},{9,10},{10,11},{11... | collective-permute-start | bytes 2457608 | tf_op jit(solution)/shard_map/ppermute | solution.py:15
  105.5 0.3 fusion.9
  105.9 0.3 fusion.8
  106.2 0.3 fusion.7
  106.6 7.9 %collective-permute-done.3 = bf16[5,640,128]{1,2,0:T(8,128)(2,1)S(1)} collective-permute-done((bf16[5,640,128]{1,2,0:T(8,128)(2,1)S(1)}, bf16[5,640,128]{1,2,0:T(8,128)(2,1)S(1)}, u32[]{:S(2)}, u32[]{:S(2)}) %collective-permute-start.3) | collective-permute-done | bytes 819232 | tf_op jit(solution)/shard_map/ppermute | solution.py:15
  114.5 0.3 fusion.6
  114.8 0.1 fusion.24
  114.9 3.2 %copy-done = f32[5,640,640]{1,2,0:T(8,128)} copy-done((f32[5,640,640]{1,2,0:T(8,128)}, f32[5,640,640]{1,2,0:T(8,128)S(1)}, u32[]{:S(2)}) %copy-start) | copy-done | bytes 8192024
  118.1 2.1 add_select_fusion
  120.2 5.8 %scatter-add.35 = f32[5,640,640]{1,2,0:T(8,128)} dynamic-update-slice(f32[5,640,640]{1,2,0:T(8,128)} %copy-done, f32[5,128,128]{1,2,0:T(8,128)S(1)} %add_select_fusion, s32[]{:T(128)} %constant.235.clone.1, s32[]{:T(128)} %bitcast.8, s32[]{:T(128)} %bitcast.9) | dynamic-update-slice | bytes 655364 | tf_op jit(solution)/shard_map/scatter-add | solution.py:95
  126.0 1.8 fusion.23
  127.8 1.8 fusion.22
  129.5 7.3 %add_convert_fusion = bf16[5,640,640]{1,2,0:T(8,128)(2,1)S(1)} fusion(f32[5,640,640]{1,2,0:T(8,128)} %fusion.22, s32[5,640,640]{1,2,0:T(8,128)} %copy.91, f32[5]{0:T(128)S(1)} %bitcast.31), kind=kLoop, calls=%fused_computation.4 | loop fusion | flops 10240000 | bytes 20480020 | tf_op jit(solution)/shard_map/convert_element_type | solution.py:99
  136.8 0.3 fusion.42
  137.1 1.9 collective-permute-start.8
  139.1 2.5 collective-permute-start.9
  141.5 20.7 %collective-permute-done.8 = bf16[5,128,640]{1,2,0:T(8,128)(2,1)S(1)} collective-permute-done((bf16[5,128,640]{1,2,0:T(8,128)(2,1)S(1)}, bf16[5,128,640]{1,2,0:T(8,128)(2,1)S(1)}, u32[]{:S(2)}, u32[]{:S(2)}) %collective-permute-start.8) | collective-permute-done | bytes 819232 | tf_op jit(solution)/shard_map/ppermute | solution.py:26
  162.2 1.9 pad_maximum_fusion.3
  164.2 6.1 %collective-permute-start.10 = (bf16[5,896,128]{1,2,0:T(8,128)(2,1)}, bf16[5,896,128]{1,2,0:T(8,128)(2,1)}, u32[]{:S(2)}, u32[]{:S(2)}) collective-permute-start(bf16[5,896,128]{1,2,0:T(8,128)(2,1)} %get-tuple-element.122), channel_id=1, source_target_pairs={{0,1},{1,2},{2,3},{3,4},{4,5},{5,6},{6,7},{8,9},{9,10},{10,11},{11... | collective-permute-start | bytes 3440648 | tf_op jit(solution)/shard_map/ppermute | solution.py:26
  170.3 1.3 collective-permute-start.11
  171.6 0.1 copy.89
  171.7 10.6 %collective-permute-done.10 = bf16[5,896,128]{1,2,0:T(8,128)(2,1)} collective-permute-done((bf16[5,896,128]{1,2,0:T(8,128)(2,1)}, bf16[5,896,128]{1,2,0:T(8,128)(2,1)}, u32[]{:S(2)}, u32[]{:S(2)}) %collective-permute-start.10) | collective-permute-done | bytes 1146912 | tf_op jit(solution)/shard_map/ppermute | solution.py:26
  182.3 27.7 %collective-permute-done.11 = bf16[5,896,128]{1,2,0:T(8,128)(2,1)} collective-permute-done((bf16[5,896,128]{1,2,0:T(8,128)(2,1)}, bf16[5,896,128]{1,2,0:T(8,128)(2,1)}, u32[]{:S(2)}, u32[]{:S(2)}) %collective-permute-start.11) | collective-permute-done | bytes 1146912 | tf_op jit(solution)/shard_map/ppermute | solution.py:28
  210.0 9.9 %multiply_reduce_fusion = f32[896,512]{1,0:T(8,128)S(1)} fusion(f32[5,512]{1,0:T(8,128)S(1)} %broadcast_multiply_fusion, f32[512]{0:T(512)S(1)} %mul.154, f32[512]{0:T(512)S(1)} %mul.149, f32[512]{0:T(512)S(1)} %sub.50, f32[896]{0:T(1024)S(1)} %iota_add_fusion, bf16[5,896,128]{1,2,0:T(8,128)(2,1)} %collective-permute-done.11, ...), kind=kOutput, calls=%fused_computation | convolution fusion | flops 4157440000 | bytes 9883136 | tf_op jit(solution)/shard_map/bij,is->bjs/dot_general | solution.py:104
  220.0 7.7 %multiply_reduce_fusion.2 = (f32[5,512]{1,0:T(8,128)S(1)}, f32[896,512]{1,0:T(8,128)S(1)}) fusion(f32[896,512]{1,0:T(8,128)S(1)} %get-tuple-element.131, f32[5,512]{1,0:T(8,128)S(1)} %broadcast_multiply_fusion, f32[512]{0:T(512)S(1)} %mul.154, f32[512]{0:T(512)S(1)} %mul.149, f32[512]{0:T(512)S(1)} %sub.53, f32[896]{0:T(1024)S(1)} %iota_add_fusion, ...), kind=kOutput, calls=%fused_computation.2 | convolution fusion | flops 4162024960 | bytes 11728384 | tf_op jit(solution)/shard_map/bij,js->bis/dot_general | solution.py:101
  227.7 2.2 multiply_reduce_fusion.6
  230.0 0.1 add.118
  230.1 0.1 concatenate.57
  230.3 0.1 concatenate.58
  230.5 0.3 reduce_sum.79
  230.9 0.1 copy.94
  231.0 0.2 copy.98
  231.2 21.9 %all_to_all.18 = f32[8,128,4]{0,2,1:T(4,128)S(1)} all-to-all(f32[8,128,4]{0,2,1:T(4,128)S(1)} %copy.98), channel_id=1, replica_groups=mesh['ra'=16,'dec'=8] {'ra','dec'}, dimensions={1} | all-to-all | bytes 32768 | tf_op jit(solution)/shard_map/all_to_all | solution.py:118
  253.1 1.0 fusion.20
  (42 shorter events, 0.7 us)
Async XLA Ops:
  3.8 23.8 %all-to-all-start = ((f32[9,128,4]{0,2,1:T(4,128)}), f32[9,128,4]{0,2,1:T(4,128)S(1)}, u32[]{:S(2)}, u32[]{:S(2)}) async-start(f32[9,128,4]{0,2,1:T(4,128)} %bitcast.4), calls=%async_computation | async-start | bytes 524288 | tf_op jit(solution)/shard_map/all_to_all | solution.py:62
  36.1 15.6 %collective-permute-start.5 = (bf16[5,128,256]{1,2,0:T(8,128)(2,1)S(1)}, bf16[5,128,256]{1,2,0:T(8,128)(2,1)S(1)}, u32[]{:S(2)}, u32[]{:S(2)}) collective-permute-start(bf16[5,128,256]{1,2,0:T(8,128)(2,1)S(1)} %pad_maximum_fusion.5), channel_id=1, source_target_pairs={{0,8},{8,16},{16,24},{24,32},{32,40},{40,48},{48,56},{56,64},{64,7... | collective-permute-start | bytes 983048 | tf_op jit(solution)/shard_map/ppermute | solution.py:15
  41.2 10.5 %collective-permute-start.4 = (bf16[5,128,256]{1,2,0:T(8,128)(2,1)S(1)}, bf16[5,128,256]{1,2,0:T(8,128)(2,1)S(1)}, u32[]{:S(2)}, u32[]{:S(2)}) collective-permute-start(bf16[5,128,256]{1,2,0:T(8,128)(2,1)S(1)} %pad_maximum_fusion.4), channel_id=1, source_target_pairs={{8,0},{16,8},{24,16},{32,24},{40,32},{48,40},{56,48},{64,56},{72,6... | collective-permute-start | bytes 983048 | tf_op jit(solution)/shard_map/ppermute | solution.py:15
  43.3 62.5 %collective-permute-start.1 = (bf16[5,128,640]{1,2,0:T(8,128)(2,1)S(1)}, bf16[5,128,640]{1,2,0:T(8,128)(2,1)S(1)}, u32[]{:S(2)}, u32[]{:S(2)}) collective-permute-start(bf16[5,128,640]{1,2,0:T(8,128)(2,1)S(1)} %get-tuple-element.120), channel_id=1, source_target_pairs={{0,8},{8,16},{16,24},{24,32},{32,40},{40,48},{48,56},{56,64},{64,7... | collective-permute-start | bytes 2457608 | tf_op jit(solution)/shard_map/ppermute | solution.py:15
  48.5 57.0 %collective-permute-start = (bf16[5,128,640]{1,2,0:T(8,128)(2,1)S(1)}, bf16[5,128,640]{1,2,0:T(8,128)(2,1)S(1)}, u32[]{:S(2)}, u32[]{:S(2)}) collective-permute-start(bf16[5,128,640]{1,2,0:T(8,128)(2,1)S(1)} %get-tuple-element.121), channel_id=1, source_target_pairs={{8,0},{16,8},{24,16},{32,24},{40,32},{48,40},{56,48},{64,56},{72,6... | collective-permute-start | bytes 2457608 | tf_op jit(solution)/shard_map/ppermute | solution.py:15
  50.4 55.8 %collective-permute-start.2 = (bf16[5,640,128]{1,2,0:T(8,128)(2,1)S(1)}, bf16[5,640,128]{1,2,0:T(8,128)(2,1)S(1)}, u32[]{:S(2)}, u32[]{:S(2)}) collective-permute-start(bf16[5,640,128]{1,2,0:T(8,128)(2,1)S(1)} %get-tuple-element.119), channel_id=1, source_target_pairs={{1,0},{2,1},{3,2},{4,3},{5,4},{6,5},{7,6},{9,8},{10,9},{11,10},{12... | collective-permute-start | bytes 2457608 | tf_op jit(solution)/shard_map/ppermute | solution.py:15
  51.9 50.0 %collective-permute-start.6 = (bf16[5,256,128]{1,2,0:T(8,128)(2,1)S(1)}, bf16[5,256,128]{1,2,0:T(8,128)(2,1)S(1)}, u32[]{:S(2)}, u32[]{:S(2)}) collective-permute-start(bf16[5,256,128]{1,2,0:T(8,128)(2,1)S(1)} %pad_maximum_fusion.6), channel_id=1, source_target_pairs={{1,0},{2,1},{3,2},{4,3},{5,4},{6,5},{7,6},{9,8},{10,9},{11,10},{12... | collective-permute-start | bytes 983048 | tf_op jit(solution)/shard_map/ppermute | solution.py:15
  53.2 52.3 %collective-permute-start.7 = (bf16[5,256,128]{1,2,0:T(8,128)(2,1)S(1)}, bf16[5,256,128]{1,2,0:T(8,128)(2,1)S(1)}, u32[]{:S(2)}, u32[]{:S(2)}) collective-permute-start(bf16[5,256,128]{1,2,0:T(8,128)(2,1)S(1)} %pad_maximum_fusion.7), channel_id=1, source_target_pairs={{0,1},{1,2},{2,3},{3,4},{4,5},{5,6},{6,7},{8,9},{9,10},{10,11},{11... | collective-permute-start | bytes 983048 | tf_op jit(solution)/shard_map/ppermute | solution.py:15
  101.8 12.6 %collective-permute-start.3 = (bf16[5,640,128]{1,2,0:T(8,128)(2,1)S(1)}, bf16[5,640,128]{1,2,0:T(8,128)(2,1)S(1)}, u32[]{:S(2)}, u32[]{:S(2)}) collective-permute-start(bf16[5,640,128]{1,2,0:T(8,128)(2,1)S(1)} %get-tuple-element.118), channel_id=1, source_target_pairs={{0,1},{1,2},{2,3},{3,4},{4,5},{5,6},{6,7},{8,9},{9,10},{10,11},{11... | collective-permute-start | bytes 2457608 | tf_op jit(solution)/shard_map/ppermute | solution.py:15
  114.9 3.2 %copy-start = (f32[5,640,640]{1,2,0:T(8,128)}, f32[5,640,640]{1,2,0:T(8,128)S(1)}, u32[]{:S(2)}) copy-start(f32[5,640,640]{1,2,0:T(8,128)S(1)} %fusion.24) | copy-start | bytes 24576004
  114.9 14.7 %copy-start.7 = (f32[1,1,5]{2,1,0:T(1,128)S(1)}, f32[1,1,5]{2,1,0:T(1,128)}, u32[]{:S(2)}) copy-start(f32[1,1,5]{2,1,0:T(1,128)} %param.26) | copy-start | bytes 64
  136.8 27.3 %copy-start.1 = (bf16[5,640,640]{1,2,0:T(8,128)(2,1)}, bf16[5,640,640]{1,2,0:T(8,128)(2,1)S(1)}, u32[]{:S(2)}) copy-start(bf16[5,640,640]{1,2,0:T(8,128)(2,1)S(1)} %add_convert_fusion) | copy-start | bytes 12288004
  137.1 25.1 %collective-permute-start.8 = (bf16[5,128,640]{1,2,0:T(8,128)(2,1)S(1)}, bf16[5,128,640]{1,2,0:T(8,128)(2,1)S(1)}, u32[]{:S(2)}, u32[]{:S(2)}) collective-permute-start(bf16[5,128,640]{1,2,0:T(8,128)(2,1)S(1)} %get-tuple-element.124), channel_id=1, source_target_pairs={{0,8},{8,16},{16,24},{24,32},{32,40},{40,48},{48,56},{56,64},{64,7... | collective-permute-start | bytes 2457608 | tf_op jit(solution)/shard_map/ppermute | solution.py:26
  139.1 23.2 %collective-permute-start.9 = (bf16[5,128,640]{1,2,0:T(8,128)(2,1)S(1)}, bf16[5,128,640]{1,2,0:T(8,128)(2,1)S(1)}, u32[]{:S(2)}, u32[]{:S(2)}) collective-permute-start(bf16[5,128,640]{1,2,0:T(8,128)(2,1)S(1)} %get-tuple-element.125), channel_id=1, source_target_pairs={{8,0},{16,8},{24,16},{32,24},{40,32},{48,40},{56,48},{64,56},{72,6... | collective-permute-start | bytes 2457608 | tf_op jit(solution)/shard_map/ppermute | solution.py:28
  162.2 1.9 copy-start.3
  162.2 1.9 copy-start.5
  164.2 18.2 %collective-permute-start.10 = (bf16[5,896,128]{1,2,0:T(8,128)(2,1)}, bf16[5,896,128]{1,2,0:T(8,128)(2,1)}, u32[]{:S(2)}, u32[]{:S(2)}) collective-permute-start(bf16[5,896,128]{1,2,0:T(8,128)(2,1)} %get-tuple-element.122), channel_id=1, source_target_pairs={{0,1},{1,2},{2,3},{3,4},{4,5},{5,6},{6,7},{8,9},{9,10},{10,11},{11... | collective-permute-start | bytes 3440648 | tf_op jit(solution)/shard_map/ppermute | solution.py:26
  170.3 39.8 %collective-permute-start.11 = (bf16[5,896,128]{1,2,0:T(8,128)(2,1)}, bf16[5,896,128]{1,2,0:T(8,128)(2,1)}, u32[]{:S(2)}, u32[]{:S(2)}) collective-permute-start(bf16[5,896,128]{1,2,0:T(8,128)(2,1)} %get-tuple-element.123), channel_id=1, source_target_pairs={{1,0},{2,1},{3,2},{4,3},{5,4},{6,5},{7,6},{9,8},{10,9},{11,10},{12... | collective-permute-start | bytes 3440648 | tf_op jit(solution)/shard_map/ppermute | solution.py:28
  171.7 48.3 %copy-start.2 = (bf16[5,640,640]{1,2,0:T(8,128)(2,1)S(1)}, bf16[5,640,640]{1,2,0:T(8,128)(2,1)}, u32[]{:S(2)}) copy-start(bf16[5,640,640]{1,2,0:T(8,128)(2,1)} %copy-done.1) | copy-start | bytes 12288004
  171.7 48.3 %copy-start.4 = (bf16[5,128,640]{1,2,0:T(8,128)(2,1)S(1)}, bf16[5,128,640]{1,2,0:T(8,128)(2,1)}, u32[]{:S(2)}) copy-start(bf16[5,128,640]{1,2,0:T(8,128)(2,1)} %copy-done.3) | copy-start | bytes 2457604
  171.7 48.3 %copy-start.6 = (bf16[5,128,640]{1,2,0:T(8,128)(2,1)S(1)}, bf16[5,128,640]{1,2,0:T(8,128)(2,1)}, u32[]{:S(2)}) copy-start(bf16[5,128,640]{1,2,0:T(8,128)(2,1)} %copy-done.5) | copy-start | bytes 2457604
where the time goes:
time: 255 us; the launch traced here: 254 us
  waiting for transfers between devices  110 us (43%)
  starting transfers between devices  48.1 us (19%)
  matrix products  25.9 us (10%)
  other arithmetic  24.2 us (9%)
  local copies, waits for them, and re-layouts  23.2 us (9%)
  blocking collectives  21.9 us (9%)
    ppermute x8, waiting for transfers between devices, passed_along(): lax.ppermute(value, axis, [(source, source + steps) for source in range(l...  51.3 us
    ppermute x2, waiting for transfers between devices, with_halo(): lax.ppermute(tail, axis, [(i, (i + 1) % count) for i in range(ends)])  31.4 us
    ppermute x2, waiting for transfers between devices, with_halo(): lax.ppermute(head, axis, [((i + 1) % count, i) for i in range(ends)])  27.7 us
    ppermute x8, starting transfers between devices, passed_along(): lax.ppermute(value, axis, [(source, source + steps) for source in range(l...  24.8 us
    all_to_all x1, blocking collectives, on_device(): lax.all_to_all(slot_grad, ('ra', 'dec'), split_axis=1, concat_axis=1, til...  21.9 us
    unnamed x18, local copies, waits for them, and re-layouts  13.6 us
    all_to_all x1, starting transfers between devices, on_device(): lax.all_to_all(outgoing, ('ra', 'dec'), split_axis=1, concat_axis=1, tile...  11.5 us
    dot_general x1, matrix products, on_device(): jnp.einsum('bij,is->bjs', weight_canvas, row_bf, preferred_element_type=j...  9.9 us
  transfers between devices with their start and end apart: 13, of which 5 were waited for; matrix products, arithmetic and copies ran while one was open for 6% of the time, Pallas kernels for 0%

commit v1 on v0

v1 whole, which is shorter than its diff:
```python
import functools
import math

import jax
import jax.numpy as jnp
from jax import lax
from jax.experimental import pallas as pl
from jax.experimental.pallas import tpu as pltpu
from jax.sharding import PartitionSpec as P

F32 = jnp.float32
BF16 = jnp.bfloat16
MESH = pl.DeviceIdType.MESH
VMEM = pl.BlockSpec(memory_space=pltpu.VMEM)

EDGE = 128
RANKS = 4
LANES = 128
HALF_LOG2E = 0.5 * math.log2(math.e)
ROOT_2PI = math.sqrt(2.0 * math.pi)


def split3(x):
    hi = x.astype(BF16)
    rest = x - hi.astype(F32)
    mid = rest.astype(BF16)
    lo = (rest - mid.astype(F32)).astype(BF16)
    return hi, mid, lo


def dot_tt(a, b):
    return lax.dot_general(a, b, (((1,), (1,)), ((), ())), preferred_element_type=F32)


def dot_nn(a, b):
    return lax.dot_general(a, b, (((1,), (0,)), ((), ())), preferred_element_type=F32)


def ranks_of(tile):
    rows = tile.shape[1]
    names = lax.broadcasted_iota(jnp.int32, (LANES, rows), 0)
    onehot = names == tile
    earlier = lax.broadcasted_iota(jnp.int32, (rows, rows), 0) < lax.broadcasted_iota(
        jnp.int32, (rows, rows), 1
    )
    before = dot_nn(
        jnp.where(onehot, 1.0, 0.0).astype(BF16), jnp.where(earlier, 1.0, 0.0).astype(BF16)
    )
    rank = jnp.sum(jnp.where(onehot, before, 0.0), axis=0, keepdims=True)
    return names, rank


def barrier_signal(na, nd, a, d):
    barrier = pltpu.get_barrier_semaphore()
    for off in range(1, na):
        pl.semaphore_signal(
            barrier, inc=1, device_id=(lax.rem(a + off, na), d), device_id_type=MESH
        )
    for off in range(1, nd):
        pl.semaphore_signal(
            barrier, inc=1, device_id=(a, lax.rem(d + off, nd)), device_id_type=MESH
        )


def barrier_wait(na, nd):
    pl.semaphore_wait(pltpu.get_barrier_semaphore(), na - 1 + nd - 1)


def route_kernel(
    na, nd, flux_ref, pos_ref, width_ref, tile_ref, out_ref,
    params, first, got1, stage, got2, send1, recv1, send2, recv2,
):
    a, d = lax.axis_index("ra"), lax.axis_index("dec")
    barrier_signal(na, nd, a, d)
    params[0:5, :] = jnp.exp(flux_ref[...])
    params[5:7, :] = pos_ref[...]
    params[7:8, :] = width_ref[...]
    tile = tile_ref[...]
    rows = tile.shape[1]
    names, rank = ranks_of(tile)
    block = params[...]
    ranked = jnp.concatenate(
        [jnp.where(rank == float(k), block, 0.0) for k in range(RANKS)], axis=0
    )
    gap = jnp.zeros((LANES - ranked.shape[0] * 3, rows), BF16)
    none = jnp.zeros(ranked.shape, BF16)
    pieces = split3(ranked)
    total = None
    for n in range(3):
        hot = jnp.where(names + (n - 1) * nd == tile, 1.0, 0.0).astype(BF16)
        for piece in pieces:
            rhs = jnp.concatenate([piece if m == n else none for m in range(3)] + [gap], axis=0)
            term = dot_tt(hot, rhs)
            total = term if total is None else total + term
    first[...] = total.reshape(na, nd, LANES)
    barrier_wait(na, nd)

    sends = []
    for off in range(1, na):
        peer = lax.rem(a + off, na)
        copy = pltpu.make_async_remote_copy(
            src_ref=first.at[peer], dst_ref=got1.at[a], send_sem=send1.at[off],
            recv_sem=recv1.at[a], device_id=(peer, d), device_id_type=MESH,
        )
        copy.start()
        sends.append(copy)
    got1[a] = first[a]
    stage[0] = jnp.zeros((na, LANES), F32)
    stage[nd + 1] = jnp.zeros((na, LANES), F32)
    for off in range(1, na):
        peer = lax.rem(a + off, na)
        pltpu.make_async_remote_copy(
            src_ref=got1.at[peer], dst_ref=got1.at[peer], send_sem=send1.at[off],
            recv_sem=recv1.at[peer], device_id=(peer, d), device_id_type=MESH,
        ).wait_recv()
    for col in range(nd):
        stage[col + 1] = got1[:, col, :]
    for off in range(1, nd):
        peer = lax.rem(d + off, nd)
        copy = pltpu.make_async_remote_copy(
            src_ref=stage.at[pl.ds(peer, 3)], dst_ref=got2.at[d], send_sem=send2.at[off],
            recv_sem=recv2.at[d], device_id=(a, peer), device_id_type=MESH,
        )
        copy.start()
        sends.append(copy)
    got2[d] = stage[pl.ds(d, 3)]
    for off in range(1, nd):
        peer = lax.rem(d + off, nd)
        pltpu.make_async_remote_copy(
            src_ref=stage.at[pl.ds(peer, 3)], dst_ref=got2.at[peer], send_sem=send2.at[off],
            recv_sem=recv2.at[peer], device_id=(a, peer), device_id_type=MESH,
        ).wait_recv()
    for n in range(3):
        out_ref[n] = got2[:, n].reshape(na * nd, LANES).T
    for copy in sends:
        copy.wait_send()


def return_kernel(
    na, nd, grad_ref, tile_ref, out_ref,
    first, got1, stage, got2, send1, recv1, send2, recv2,
):
    a, d = lax.axis_index("ra"), lax.axis_index("dec")
    barrier_signal(na, nd, a, d)
    for n in range(3):
        first[:, n] = grad_ref[n].T.reshape(nd, na, LANES)
    got1[nd] = jnp.zeros(got1.shape[1:], F32)
    got1[nd + 1] = jnp.zeros(got1.shape[1:], F32)
    got2[na] = jnp.zeros(got2.shape[1:], F32)
    got2[na + 1] = jnp.zeros(got2.shape[1:], F32)
    tile = tile_ref[...]
    names, rank = ranks_of(tile)
    hot = jnp.where(names == tile, 1.0, 0.0).astype(BF16)
    barrier_wait(na, nd)

    sends = []
    for off in range(1, nd):
        peer = lax.rem(d + off, nd)
        copy = pltpu.make_async_remote_copy(
            src_ref=first.at[peer], dst_ref=got1.at[d], send_sem=send1.at[off],
            recv_sem=recv1.at[d], device_id=(a, peer), device_id_type=MESH,
        )
        copy.start()
        sends.append(copy)
    got1[d] = first[d]
    for off in range(1, nd):
        peer = lax.rem(d + off, nd)
        pltpu.make_async_remote_copy(
            src_ref=first.at[peer], dst_ref=got1.at[peer], send_sem=send1.at[off],
            recv_sem=recv1.at[peer], device_id=(a, peer), device_id_type=MESH,
        ).wait_recv()
    for col in range(nd):
        after, before = (col + 1 if col + 1 < nd else nd), (col - 1 if col else nd + 1)
        stage[:, col, :] = got1[after, 0] + got1[col, 1] + got1[before, 2]
    for off in range(1, na):
        peer = lax.rem(a + off, na)
        copy = pltpu.make_async_remote_copy(
            src_ref=stage.at[peer], dst_ref=got2.at[a], send_sem=send2.at[off],
            recv_sem=recv2.at[a], device_id=(peer, d), device_id_type=MESH,
        )
        copy.start()
        sends.append(copy)
    got2[a] = stage[a]
    for off in range(1, na):
        peer = lax.rem(a + off, na)
        pltpu.make_async_remote_copy(
            src_ref=stage.at[peer], dst_ref=got2.at[peer], send_sem=send2.at[off],
            recv_sem=recv2.at[peer], device_id=(peer, d), device_id_type=MESH,
        ).wait_recv()
    mine = got2[0:na].reshape(na * nd, LANES)
    none = jnp.zeros((nd, LANES), F32)
    later = jnp.concatenate([mine[nd:], none], axis=0)
    sooner = jnp.concatenate([none, mine[:-nd]], axis=0)
    held, width = mine.T, 8 * RANKS
    slots = (
        later.T[0:width] + held[width : 2 * width] + sooner.T[2 * width : 3 * width]
    )
    rows = None
    for piece in split3(slots):
        term = dot_nn(piece, hot)
        rows = term if rows is None else rows + term
    total = None
    for k in range(RANKS):
        term = jnp.where(rank == float(k), rows[8 * k : 8 * k + 8], 0.0)
        total = term if total is None else total + term
    out_ref[...] = total
    for copy in sends:
        copy.wait_send()


CORNERS = ((-1, -1), (-1, 1), (1, -1), (1, 1))
SIDES = ((-1, 0), (1, 0), (0, -1), (0, 1))
GROUPS = CORNERS + SIDES + ((0, 0),)
BANDS = 5
STEP = 64
OUTS = BANDS + 6


def compute_kernel(
    side, src_ref, sky_ref, counts_ref, out_ref,
    counts, weights, turned, prof_i, prof_j, low_i, low_j, scaled,
    rim_top, rim_bottom, rim_left, rim_right, sums, count_sem,
):
    slots = RANKS * LANES

    def copy_in(b):
        return pltpu.make_async_copy(counts_ref.at[b], counts.at[b], count_sem.at[b])

    for b in range(BANDS):
        copy_in(b).start()
    sums[...] = jnp.zeros_like(sums)
    index = {group: n for n, group in enumerate(GROUPS)}

    def source(group, k, row):
        dr, dc = group
        start = (dr + 1) * 8 * RANKS + k * 8 + row
        return src_ref[dc + 1, start : start + 1, :]

    def span(step):
        if step == 0:
            return 0, side
        return (0, EDGE) if step < 0 else (side - EDGE, EDGE)

    def make_profile(group, axis, f32_ref, low_ref, scaled_ref):
        first, count = span(group[axis])
        base = first + 0.5 - group[axis] * side
        iota = lax.broadcasted_iota(jnp.int32, (STEP, LANES), 0).astype(F32)
        for k in range(RANKS):
            lanes = slice(k * LANES, (k + 1) * LANES)
            center = source(group, k, 5 + axis)
            inverse = 1.0 / (float(EDGE) * jnp.exp(source(group, k, 7)))
            factor = -HALF_LOG2E * inverse * inverse
            norm = inverse * (1.0 / ROOT_2PI)
            flux = [source(group, k, b) for b in range(BANDS)] if scaled_ref is not None else []

            def body(step, carry):
                start = pl.multiple_of(step * STEP, STEP)
                off = iota + (base + start.astype(F32)) - center
                prof = jnp.exp2(off * factor * off) * norm
                rows = pl.ds(start, STEP)
                f32_ref[rows, lanes] = prof
                if low_ref is not None:
                    low_ref[rows, lanes] = prof.astype(BF16)
                for b, f in enumerate(flux):
                    into = pl.ds(pl.multiple_of(b * count + step * STEP, STEP), STEP)
                    scaled_ref[into, lanes] = (prof * f).astype(BF16)
                return carry

            lax.fori_loop(0, count // STEP, body, 0)

    def rounded(x):
        return x.astype(BF16).astype(F32)

    rims_ij = {-1: rim_top, 1: rim_bottom}
    rims_ji = {-1: rim_left, 1: rim_right}
    for group in SIDES + CORNERS:
        n = index[group]
        dr, dc = group
        if dr:
            make_profile(group, 0, prof_i[n], None, scaled[n])
            make_profile(group, 1, prof_j[n], low_j[n], None)
            part = rounded(dot_tt(scaled[n][...], low_j[n][...]))
            part = part.reshape(BANDS, EDGE, part.shape[1])
            if dc == 0:
                rims_ij[dr][...] = part
            else:
                start = 0 if dc < 0 else side - EDGE
                rims_ij[dr][:, :, start : start + EDGE] += part
        else:
            make_profile(group, 0, prof_i[n], low_i[n], None)
            make_profile(group, 1, prof_j[n], None, scaled[n])
            rims_ji[dc][...] = rounded(dot_tt(low_i[n][...], scaled[n][...]))

    own = index[(0, 0)]
    make_profile((0, 0), 0, prof_i[own], low_i[own], scaled[own])
    make_profile((0, 0), 1, prof_j[own], low_j[own], None)

    for b in range(BANDS):
        model = rounded(dot_tt(scaled[own][b * side : (b + 1) * side, :], low_j[own][...]))
        copy_in(b).wait()
        level = sky_ref[0, 0, b]
        for chunk in range(side // EDGE):
            rows = slice(chunk * EDGE, (chunk + 1) * EDGE)
            for other in range(side // EDGE):
                cols = slice(other * EDGE, (other + 1) * EDGE)
                part = model[rows, cols] + level
                if other == 0:
                    part = part + rim_left[rows, b * EDGE : (b + 1) * EDGE]
                if other == side // EDGE - 1:
                    part = part + rim_right[rows, b * EDGE : (b + 1) * EDGE]
                if chunk == 0:
                    part = part + rim_top[b, :, cols]
                if chunk == side // EDGE - 1:
                    part = part + rim_bottom[b, :, cols]
                ratio = counts[b, rows, cols].astype(F32) / part - 1.0
                low = ratio.astype(BF16)
                weights[b, rows, cols] = low
                turned[cols, b * side + chunk * EDGE : b * side + (chunk + 1) * EDGE] = low.T

    def fold(x):
        return jnp.sum(x.reshape(x.shape[0] // 8, 8, x.shape[1]), axis=0)

    def moments(group, axis, k, start, total, prof, base):
        n = index[group]
        iota = lax.broadcasted_iota(jnp.int32, total.shape, 0).astype(F32)
        off = iota + (base + start) - source(group, k, 5 + axis)
        zeroth = prof * total
        once = zeroth * off
        twice = once * off
        at = BANDS + 3 * axis
        sums[n, k, at] += fold(zeroth)
        sums[n, k, at + 1] += fold(once)
        sums[n, k, at + 2] += fold(twice)

    def per_band(group, axis, lhs, rhs, prof_ref, rows, start):
        n = index[group]
        base = span(group[axis])[0] + 0.5 - group[axis] * side
        for pair in range(RANKS // 2):
            wide = slice(pair * 2 * LANES, (pair + 1) * 2 * LANES)
            along = dot_nn(lhs, rhs[:, wide])
            for k in (2 * pair, 2 * pair + 1):
                lanes = slice((k - 2 * pair) * LANES, (k - 2 * pair + 1) * LANES)
                prof = prof_ref[rows, k * LANES : (k + 1) * LANES]
                low = rounded(prof)
                total = None
                for b in range(BANDS):
                    band = along[b * EDGE : (b + 1) * EDGE, lanes]
                    sums[n, k, b] += fold(low * band)
                    term = source(group, k, b) * band
                    total = term if total is None else total + term
                moments(group, axis, k, start, total, prof, base)

    def all_bands(group, axis, lhs, scaled_ref, prof_ref):
        base = span(group[axis])[0] + 0.5 - group[axis] * side
        for pair in range(RANKS // 2):
            wide = slice(pair * 2 * LANES, (pair + 1) * 2 * LANES)
            along = dot_nn(lhs, scaled_ref[:, wide])
            for k in (2 * pair, 2 * pair + 1):
                lanes = slice((k - 2 * pair) * LANES, (k - 2 * pair + 1) * LANES)
                prof = prof_ref[:, k * LANES : (k + 1) * LANES]
                moments(group, axis, k, 0.0, along[:, lanes], prof, base)

    for group in SIDES + CORNERS:
        n = index[group]
        (r0, rn), (c0, cn) = span(group[0]), span(group[1])
        if group[0]:
            lhs = weights[:, r0 : r0 + rn, c0 : c0 + cn].reshape(BANDS * rn, cn)
            per_band(group, 0, lhs, low_j[n], prof_i[n], slice(0, EDGE), 0.0)
            lhs = jnp.concatenate(
                [turned[c0 : c0 + cn, b * side + r0 : b * side + r0 + rn] for b in range(BANDS)],
                axis=1,
            )
            all_bands(group, 1, lhs, scaled[n], prof_j[n])
        else:
            lhs = jnp.concatenate(
                [turned[c0 : c0 + cn, b * side : (b + 1) * side] for b in range(BANDS)], axis=0
            )
            per_band(group, 1, lhs, low_i[n], prof_j[n], slice(0, EDGE), 0.0)
            lhs = jnp.concatenate([weights[b, :, c0 : c0 + cn] for b in range(BANDS)], axis=1)
            all_bands(group, 0, lhs, scaled[n], prof_i[n])

    def own_chunk(chunk, carry):
        start = pl.multiple_of(chunk * EDGE, EDGE)
        lhs = weights[:, pl.ds(start, EDGE), :].reshape(BANDS * EDGE, side)
        per_band(
            (0, 0), 0, lhs, low_j[own], prof_i[own], pl.ds(start, EDGE), start.astype(F32)
        )
        return carry

    lax.fori_loop(0, side // EDGE, own_chunk, 0)
    all_bands((0, 0), 1, turned[...], scaled[own], prof_j[own])

    out_ref[...] = jnp.zeros_like(out_ref)
    for group in GROUPS:
        n, (dr, dc) = index[group], group
        for k in range(RANKS):
            inverse = 1.0 / (float(EDGE) * jnp.exp(source(group, k, 7)))
            square = inverse * inverse

            def total(which):
                return jnp.sum(sums[n, k, which], axis=0, keepdims=True)

            start = (dr + 1) * 8 * RANKS + k * 8
            for b in range(BANDS):
                out_ref[dc + 1, start + b : start + b + 1, :] = source(group, k, b) * total(b)
            zeroth = total(BANDS) + total(BANDS + 3)
            second = total(BANDS + 2) + total(BANDS + 5)
            out_ref[dc + 1, start + 5 : start + 6, :] = total(BANDS + 1) * square
            out_ref[dc + 1, start + 6 : start + 7, :] = total(BANDS + 4) * square
            out_ref[dc + 1, start + 7 : start + 8, :] = second * square - zeroth


def on_device(na, nd, log_flux, position, log_width, owner_tile, sky_level, counts):
    rows = log_flux.shape[1]
    side = counts.shape[1]
    slots = RANKS * LANES
    width = log_width.reshape(1, rows)
    tile = owner_tile.reshape(1, rows)
    dma = pltpu.SemaphoreType.DMA

    routed = pl.pallas_call(
        functools.partial(route_kernel, na, nd),
        out_shape=jax.ShapeDtypeStruct((3, LANES, na * nd), F32),
        in_specs=[VMEM] * 4,
        out_specs=VMEM,
        scratch_shapes=[
            pltpu.VMEM((8, rows), F32),
            pltpu.VMEM((na, nd, LANES), F32),
            pltpu.VMEM((na, nd, LANES), F32),
            pltpu.VMEM((nd + 2, na, LANES), F32),
            pltpu.VMEM((nd, 3, na, LANES), F32),
            dma((na,)), dma((na,)), dma((nd,)), dma((nd,)),
        ],
        compiler_params=pltpu.CompilerParams(collective_id=0, has_side_effects=True),
        name="route",
    )(log_flux, position, width, tile)

    def extent(step):
        return EDGE if step else side

    prof_i = [pltpu.VMEM((extent(g[0]), slots), F32) for g in GROUPS]
    prof_j = [pltpu.VMEM((extent(g[1]), slots), F32) for g in GROUPS]
    low_i = [pltpu.VMEM((extent(g[0]) if g[0] == 0 else 16, slots), BF16) for g in GROUPS]
    low_j = [pltpu.VMEM((extent(g[1]) if g[0] or not g[1] else 16, slots), BF16) for g in GROUPS]
    scaled = [pltpu.VMEM((BANDS * (EDGE if g != (0, 0) else side), slots), BF16) for g in GROUPS]
    partial = pl.pallas_call(
        functools.partial(compute_kernel, side),
        out_shape=jax.ShapeDtypeStruct((3, LANES, na * nd), F32),
        in_specs=[
            VMEM,
            pl.BlockSpec(memory_space=pltpu.SMEM),
            pl.BlockSpec(memory_space=pl.ANY),
        ],
        out_specs=VMEM,
        scratch_shapes=[
            pltpu.VMEM((BANDS, side, side), jnp.int32),
            pltpu.VMEM((BANDS, side, side), BF16),
            pltpu.VMEM((side, BANDS * side), BF16),
            prof_i, prof_j, low_i, low_j, scaled,
            pltpu.VMEM((BANDS, EDGE, side), F32),
            pltpu.VMEM((BANDS, EDGE, side), F32),
            pltpu.VMEM((side, BANDS * EDGE), F32),
            pltpu.VMEM((side, BANDS * EDGE), F32),
            pltpu.VMEM((len(GROUPS), RANKS, OUTS, 8, LANES), F32),
            dma((BANDS,)),
        ],
        compiler_params=pltpu.CompilerParams(vmem_limit_bytes=60 << 20),
        name="compute",
    )(routed, sky_level, counts)

    return pl.pallas_call(
        functools.partial(return_kernel, na, nd),
        out_shape=jax.ShapeDtypeStruct((8, rows), F32),
        in_specs=[VMEM] * 2,
        out_specs=VMEM,
        scratch_shapes=[
            pltpu.VMEM((nd, 3, na, LANES), F32),
            pltpu.VMEM((nd + 2, 3, na, LANES), F32),
            pltpu.VMEM((na, nd, LANES), F32),
            pltpu.VMEM((na + 2, nd, LANES), F32),
            dma((nd,)), dma((nd,)), dma((na,)), dma((na,)),
        ],
        compiler_params=pltpu.CompilerParams(collective_id=1, has_side_effects=True),
        name="give_back",
    )(partial, tile)


def solution(mesh):
    na, nd = mesh.shape["ra"], mesh.shape["dec"]
    in_specs = (
        P(None, ("ra", "dec")),
        P(None, ("ra", "dec")),
        P(("ra", "dec")),
        P(("ra", "dec"), None),
        P("ra", "dec", None),
        P(None, "ra", "dec"),
    )
    return jax.shard_map(
        functools.partial(on_device, na, nd),
        mesh=mesh,
        in_specs=in_specs,
        out_specs=P(None, ("ra", "dec")),
        check_vma=False,
    )
```

time: 255 us -> 71.5 us (0.28)
  waiting for transfers between devices: 110 us -> 0 us
  Pallas kernels: 0 us -> 70 us
  starting transfers between devices: 48.1 us -> 0 us
  matrix products: 25.9 us -> 0 us
  other arithmetic: 24.2 us -> 0 us
  local copies, waits for them, and re-layouts: 23.2 us -> 1.3 us
  blocking collectives: 21.9 us -> 0 us
    ppermute x12 -> x0, waiting for transfers between devices: 110 us -> none  [the longest x8 51.3 us: passed_along(): lax.ppermute(value, axis, [(source, source + steps) for source in range(l...]
    pallas_call x0 -> x3, Pallas kernels: none -> 70 us  [the longest x1 34.2 us: on_device(): pl.pallas_call(functools.partial(compute_kernel, side), out_shape=jax.Sha...]
    ppermute x12 -> x0, starting transfers between devices: 36.6 us -> none  [the longest x8 24.8 us: passed_along(): lax.ppermute(value, axis, [(source, source + steps) for source in range(l...]
    dot_general x5 -> x0, matrix products: 25.9 us -> none  [the longest x1 9.9 us: on_device(): jnp.einsum('bij,is->bjs', weight_canvas, row_bf, preferred_element_type=j...]
    all_to_all x1 -> x0, blocking collectives: 21.9 us -> none  [on_device(): lax.all_to_all(slot_grad, ('ra', 'dec'), split_axis=1, concat_axis=1, til...]
    unnamed x18 -> x1, local copies, waits for them, and re-layouts: 13.6 us -> 1.3 us
    all_to_all x1 -> x0, starting transfers between devices: 11.5 us -> none  [on_device(): lax.all_to_all(outgoing, ('ra', 'dec'), split_axis=1, concat_axis=1, tile...]
    convert_element_type x5 -> x0, other arithmetic: 8.42 us -> none  [the longest x1 7.27 us: on_device(): (counts.astype(jnp.float32) / intensity - 1.0).astype(jnp.bfloat16)]
  transfers between devices with their start and end apart: 13 -> 0, of which waited for: 5 -> 0; matrix products, arithmetic and copies ran while one was open for 6% -> 0% of each run, Pallas kernels for 0% -> 0%
where the time goes in v1:
time: 71.5 us; the launch traced here: 71.3 us
  Pallas kernels  70 us (98%)
  local copies, waits for them, and re-layouts  1.3 us (2%)
    pallas_call x1, Pallas kernels, on_device(): pl.pallas_call(functools.partial(compute_kernel, side), out_shape=jax.Sha...  34.2 us
    pallas_call x1, Pallas kernels, on_device(): pl.pallas_call(functools.partial(route_kernel, na, nd), out_shape=jax.Sha...  19.3 us
    pallas_call x1, Pallas kernels, on_device(): pl.pallas_call(functools.partial(return_kernel, na, nd), out_shape=jax.Sh...  16.5 us

profile of v1, /device:TPU:1, one launch (start us, length us, event | category | flops | bytes accessed | tf_op | source)
XLA Modules:
  0.0 71.3 jit_solution(7712527241237675547)
XLA Ops:
  0.0 19.3 %route.1.src_ref = f32[3,128,128]{2,1,0:T(8,128)} custom-call(f32[5,256]{1,0:T(8,128)} %flux_ref.1, f32[2,256]{1,0:T(2,128)} %pos_ref.1, f32[1,256]{1,0:T(1,128)} %bitcast.4, s32[1,256]{1,0:T(1,128)} %bitcast.2), custom_call_target="tpu_custom_call" | custom-call | tf_op jit(solution)/shard_map/route/pallas_call | solution.py:421
  19.3 34.2 %compute.1.grad_ref = f32[3,128,128]{2,1,0:T(8,128)} custom-call(f32[3,128,128]{2,1,0:T(8,128)} %route.1.src_ref, f32[1,1,5]{2,1,0:T(1,128)} %sky_ref.1, s32[5,640,640]{2,1,0:T(8,128)} %counts_ref.1), custom_call_target="tpu_custom_call" | custom-call | tf_op jit(solution)/shard_map/compute/pallas_call | solution.py:446
  53.5 16.5 %give_back.1 = f32[8,256]{1,0:T(8,128)} custom-call(f32[3,128,128]{2,1,0:T(8,128)} %compute.1.grad_ref, s32[1,256]{1,0:T(1,128)} %bitcast.3), custom_call_target="tpu_custom_call" | custom-call | tf_op jit(solution)/shard_map/give_back/pallas_call | solution.py:471
  70.0 1.3 %copy.8 = f32[8,256]{1,0:T(8,128)} copy(f32[8,256]{1,0:T(8,128)} %give_back.1) | data formatting | bytes 16384

commit v2 on v1

--- a/solution.py
+++ b/solution.py
@@ -228,7 +228,6 @@
 
     for b in range(BANDS):
         copy_in(b).start()
-    sums[...] = jnp.zeros_like(sums)
     index = {group: n for n, group in enumerate(GROUPS)}
 
     def source(group, k, row):
@@ -266,7 +265,7 @@
                     scaled_ref[into, lanes] = (prof * f).astype(BF16)
                 return carry
 
-            lax.fori_loop(0, count // STEP, body, 0)
+            lax.fori_loop(0, count // STEP, body, 0, unroll=True)
 
     def rounded(x):
         return x.astype(BF16).astype(F32)
@@ -320,19 +319,36 @@
     def fold(x):
         return jnp.sum(x.reshape(x.shape[0] // 8, 8, x.shape[1]), axis=0)
 
-    def moments(group, axis, k, start, total, prof, base):
+    def put(n, k, at, value, add):
+        if add:
+            sums[n, k, at] += value
+        else:
+            sums[n, k, at] = value
+
+    def moments(group, axis, k, start, total, prof, base, add):
         n = index[group]
-        iota = lax.broadcasted_iota(jnp.int32, total.shape, 0).astype(F32)
-        off = iota + (base + start) - source(group, k, 5 + axis)
-        zeroth = prof * total
-        once = zeroth * off
-        twice = once * off
+        iota = lax.broadcasted_iota(jnp.int32, (8, LANES), 0).astype(F32)
+        zeroth = first = second = None
+        for run in range(total.shape[0] // EDGE):
+            s0 = s1 = s2 = None
+            for row in range(run * EDGE, (run + 1) * EDGE, 8):
+                term = prof[row : row + 8] * total[row : row + 8]
+                s0 = term if s0 is None else s0 + term
+                s1 = s0 if s1 is None else s1 + s0
+                s2 = s1 if s2 is None else s2 + s1
+            end = iota + (base + (start + (run + 1) * EDGE)) - source(group, k, 5 + axis)
+            scaled0 = end * s0
+            one = scaled0 - 8.0 * s1
+            two = end * (scaled0 - 16.0 * s1) + 64.0 * (s2 + (s2 - s1))
+            zeroth = s0 if zeroth is None else zeroth + s0
+            first = one if first is None else first + one
+            second = two if second is None else second + two
         at = BANDS + 3 * axis
-        sums[n, k, at] += fold(zeroth)
-        sums[n, k, at + 1] += fold(once)
-        sums[n, k, at + 2] += fold(twice)
-
-    def per_band(group, axis, lhs, rhs, prof_ref, rows, start):
+        put(n, k, at, zeroth, add)
+        put(n, k, at + 1, first, add)
+        put(n, k, at + 2, second, add)
+
+    def per_band(group, axis, lhs, rhs, prof_ref, start, add):
         n = index[group]
         base = span(group[axis])[0] + 0.5 - group[axis] * side
         for pair in range(RANKS // 2):
@@ -340,15 +356,15 @@
             along = dot_nn(lhs, rhs[:, wide])
             for k in (2 * pair, 2 * pair + 1):
                 lanes = slice((k - 2 * pair) * LANES, (k - 2 * pair + 1) * LANES)
-                prof = prof_ref[rows, k * LANES : (k + 1) * LANES]
+                prof = prof_ref[start : start + EDGE, k * LANES : (k + 1) * LANES]
                 low = rounded(prof)
                 total = None
                 for b in range(BANDS):
                     band = along[b * EDGE : (b + 1) * EDGE, lanes]
-                    sums[n, k, b] += fold(low * band)
+                    put(n, k, b, fold(low * band), add)
                     term = source(group, k, b) * band
                     total = term if total is None else total + term
-                moments(group, axis, k, start, total, prof, base)
+                moments(group, axis, k, start, total, prof, base, add)
 
     def all_bands(group, axis, lhs, scaled_ref, prof_ref):
         base = span(group[axis])[0] + 0.5 - group[axis] * side
@@ -358,14 +374,14 @@
             for k in (2 * pair, 2 * pair + 1):
                 lanes = slice((k - 2 * pair) * LANES, (k - 2 * pair + 1) * LANES)
                 prof = prof_ref[:, k * LANES : (k + 1) * LANES]
-                moments(group, axis, k, 0.0, along[:, lanes], prof, base)
+                moments(group, axis, k, 0, along[:, lanes], prof, base, False)
 
     for group in SIDES + CORNERS:
         n = index[group]
         (r0, rn), (c0, cn) = span(group[0]), span(group[1])
         if group[0]:
             lhs = weights[:, r0 : r0 + rn, c0 : c0 + cn].reshape(BANDS * rn, cn)
-            per_band(group, 0, lhs, low_j[n], prof_i[n], slice(0, EDGE), 0.0)
+            per_band(group, 0, lhs, low_j[n], prof_i[n], 0, False)
             lhs = jnp.concatenate(
                 [turned[c0 : c0 + cn, b * side + r0 : b * side + r0 + rn] for b in range(BANDS)],
                 axis=1,
@@ -375,19 +391,13 @@
             lhs = jnp.concatenate(
                 [turned[c0 : c0 + cn, b * side : (b + 1) * side] for b in range(BANDS)], axis=0
             )
-            per_band(group, 1, lhs, low_i[n], prof_j[n], slice(0, EDGE), 0.0)
+            per_band(group, 1, lhs, low_i[n], prof_j[n], 0, False)
             lhs = jnp.concatenate([weights[b, :, c0 : c0 + cn] for b in range(BANDS)], axis=1)
             all_bands(group, 0, lhs, scaled[n], prof_i[n])
 
-    def own_chunk(chunk, carry):
-        start = pl.multiple_of(chunk * EDGE, EDGE)
-        lhs = weights[:, pl.ds(start, EDGE), :].reshape(BANDS * EDGE, side)
-        per_band(
-            (0, 0), 0, lhs, low_j[own], prof_i[own], pl.ds(start, EDGE), start.astype(F32)
-        )
-        return carry
-
-    lax.fori_loop(0, side // EDGE, own_chunk, 0)
+    for start in range(0, side, EDGE):
+        lhs = weights[:, start : start + EDGE, :].reshape(BANDS * EDGE, side)
+        per_band((0, 0), 0, lhs, low_j[own], prof_i[own], start, start > 0)
     all_bands((0, 0), 1, turned[...], scaled[own], prof_j[own])
 
     out_ref[...] = jnp.zeros_like(out_ref)
@@ -410,30 +420,9 @@
             out_ref[dc + 1, start + 7 : start + 8, :] = second * square - zeroth
 
 
-def on_device(na, nd, log_flux, position, log_width, owner_tile, sky_level, counts):
-    rows = log_flux.shape[1]
-    side = counts.shape[1]
+def compute_call(side, na, nd, routed, sky_level, counts):
     slots = RANKS * LANES
-    width = log_width.reshape(1, rows)
-    tile = owner_tile.reshape(1, rows)
     dma = pltpu.SemaphoreType.DMA
-
-    routed = pl.pallas_call(
-        functools.partial(route_kernel, na, nd),
-        out_shape=jax.ShapeDtypeStruct((3, LANES, na * nd), F32),
-        in_specs=[VMEM] * 4,
-        out_specs=VMEM,
-        scratch_shapes=[
-            pltpu.VMEM((8, rows), F32),
-            pltpu.VMEM((na, nd, LANES), F32),
-            pltpu.VMEM((na, nd, LANES), F32),
-            pltpu.VMEM((nd + 2, na, LANES), F32),
-            pltpu.VMEM((nd, 3, na, LANES), F32),
-            dma((na,)), dma((na,)), dma((nd,)), dma((nd,)),
-        ],
-        compiler_params=pltpu.CompilerParams(collective_id=0, has_side_effects=True),
-        name="route",
-    )(log_flux, position, width, tile)
 
     def extent(step):
         return EDGE if step else side
@@ -443,7 +432,7 @@
     low_i = [pltpu.VMEM((extent(g[0]) if g[0] == 0 else 16, slots), BF16) for g in GROUPS]
     low_j = [pltpu.VMEM((extent(g[1]) if g[0] or not g[1] else 16, slots), BF16) for g in GROUPS]
     scaled = [pltpu.VMEM((BANDS * (EDGE if g != (0, 0) else side), slots), BF16) for g in GROUPS]
-    partial = pl.pallas_call(
+    return pl.pallas_call(
         functools.partial(compute_kernel, side),
         out_shape=jax.ShapeDtypeStruct((3, LANES, na * nd), F32),
         in_specs=[
@@ -468,6 +457,33 @@
         name="compute",
     )(routed, sky_level, counts)
 
+
+def on_device(na, nd, log_flux, position, log_width, owner_tile, sky_level, counts):
+    rows = log_flux.shape[1]
+    side = counts.shape[1]
+    width = log_width.reshape(1, rows)
+    tile = owner_tile.reshape(1, rows)
+    dma = pltpu.SemaphoreType.DMA
+
+    routed = pl.pallas_call(
+        functools.partial(route_kernel, na, nd),
+        out_shape=jax.ShapeDtypeStruct((3, LANES, na * nd), F32),
+        in_specs=[VMEM] * 4,
+        out_specs=VMEM,
+        scratch_shapes=[
+            pltpu.VMEM((8, rows), F32),
+            pltpu.VMEM((na, nd, LANES), F32),
+            pltpu.VMEM((na, nd, LANES), F32),
+            pltpu.VMEM((nd + 2, na, LANES), F32),
+            pltpu.VMEM((nd, 3, na, LANES), F32),
+            dma((na,)), dma((na,)), dma((nd,)), dma((nd,)),
+        ],
+        compiler_params=pltpu.CompilerParams(collective_id=0, has_side_effects=True),
+        name="route",
+    )(log_flux, position, width, tile)
+
+    partial = compute_call(side, na, nd, routed, sky_level, counts)
+
     return pl.pallas_call(
         functools.partial(return_kernel, na, nd),
         out_shape=jax.ShapeDtypeStruct((8, rows), F32),

time: 71.5 us -> 59.9 us (0.84)
  Pallas kernels: 70 us -> 58.4 us
    pallas_call x1, Pallas kernels: 34.2 us -> 22.6 us  [compute_call(): pl.pallas_call(functools.partial(compute_kernel, side), out_shape=jax.Sha...]
where the time goes in v2:
time: 59.9 us; the launch traced here: 59.7 us
  Pallas kernels  58.4 us (97%)
  local copies, waits for them, and re-layouts  1.3 us (2%)
    pallas_call x1, Pallas kernels, compute_call(): pl.pallas_call(functools.partial(compute_kernel, side), out_shape=jax.Sha...  22.6 us
    pallas_call x1, Pallas kernels, on_device(): pl.pallas_call(functools.partial(route_kernel, na, nd), out_shape=jax.Sha...  19.3 us
    pallas_call x1, Pallas kernels, on_device(): pl.pallas_call(functools.partial(return_kernel, na, nd), out_shape=jax.Sh...  16.5 us
    unnamed x1, local copies, waits for them, and re-layouts  1.3 us

profile of v2, /device:TPU:1, one launch (start us, length us, event | category | flops | bytes accessed | tf_op | source)
XLA Modules:
  0.0 59.7 jit_solution(1418722654406534615)
XLA Ops:
  0.0 19.3 %route.1.src_ref = f32[3,128,128]{2,1,0:T(8,128)} custom-call(f32[5,256]{1,0:T(8,128)} %flux_ref.1, f32[2,256]{1,0:T(2,128)} %pos_ref.1, f32[1,256]{1,0:T(1,128)} %bitcast.4, s32[1,256]{1,0:T(1,128)} %bitcast.2), custom_call_target="tpu_custom_call" | custom-call | tf_op jit(solution)/shard_map/route/pallas_call | solution.py:468
  19.3 22.6 %compute.1.grad_ref = f32[3,128,128]{2,1,0:T(8,128)} custom-call(f32[3,128,128]{2,1,0:T(8,128)} %route.1.src_ref, f32[1,1,5]{2,1,0:T(1,128)} %sky_ref.1, s32[5,640,640]{2,1,0:T(8,128)} %counts_ref.1), custom_call_target="tpu_custom_call" | custom-call | tf_op jit(solution)/shard_map/compute/pallas_call | solution.py:435
  41.9 16.5 %give_back.1 = f32[8,256]{1,0:T(8,128)} custom-call(f32[3,128,128]{2,1,0:T(8,128)} %compute.1.grad_ref, s32[1,256]{1,0:T(1,128)} %bitcast.3), custom_call_target="tpu_custom_call" | custom-call | tf_op jit(solution)/shard_map/give_back/pallas_call | solution.py:487
  58.4 1.3 %copy.8 = f32[8,256]{1,0:T(8,128)} copy(f32[8,256]{1,0:T(8,128)} %give_back.1) | data formatting | bytes 16384

commit v3 on v2

--- a/solution.py
+++ b/solution.py
@@ -66,7 +66,7 @@
     pl.semaphore_wait(pltpu.get_barrier_semaphore(), na - 1 + nd - 1)
 
 
-def route_kernel(
+def route(
     na, nd, flux_ref, pos_ref, width_ref, tile_ref, out_ref,
     params, first, got1, stage, got2, send1, recv1, send2, recv2,
 ):
@@ -132,26 +132,16 @@
         ).wait_recv()
     for n in range(3):
         out_ref[n] = got2[:, n].reshape(na * nd, LANES).T
-    for copy in sends:
-        copy.wait_send()
-
-
-def return_kernel(
+    return sends
+
+
+def give_back(
     na, nd, grad_ref, tile_ref, out_ref,
     first, got1, stage, got2, send1, recv1, send2, recv2,
 ):
     a, d = lax.axis_index("ra"), lax.axis_index("dec")
-    barrier_signal(na, nd, a, d)
     for n in range(3):
         first[:, n] = grad_ref[n].T.reshape(nd, na, LANES)
-    got1[nd] = jnp.zeros(got1.shape[1:], F32)
-    got1[nd + 1] = jnp.zeros(got1.shape[1:], F32)
-    got2[na] = jnp.zeros(got2.shape[1:], F32)
-    got2[na + 1] = jnp.zeros(got2.shape[1:], F32)
-    tile = tile_ref[...]
-    names, rank = ranks_of(tile)
-    hot = jnp.where(names == tile, 1.0, 0.0).astype(BF16)
-    barrier_wait(na, nd)
 
     sends = []
     for off in range(1, nd):
@@ -170,8 +160,12 @@
             recv_sem=recv1.at[peer], device_id=(a, peer), device_id_type=MESH,
         ).wait_recv()
     for col in range(nd):
-        after, before = (col + 1 if col + 1 < nd else nd), (col - 1 if col else nd + 1)
-        stage[:, col, :] = got1[after, 0] + got1[col, 1] + got1[before, 2]
+        part = got1[col, 1]
+        if col + 1 < nd:
+            part = part + got1[col + 1, 0]
+        if col:
+            part = part + got1[col - 1, 2]
+        stage[:, col, :] = part
     for off in range(1, na):
         peer = lax.rem(a + off, na)
         copy = pltpu.make_async_remote_copy(
@@ -187,7 +181,10 @@
             src_ref=stage.at[peer], dst_ref=got2.at[peer], send_sem=send2.at[off],
             recv_sem=recv2.at[peer], device_id=(peer, d), device_id_type=MESH,
         ).wait_recv()
-    mine = got2[0:na].reshape(na * nd, LANES)
+    tile = tile_ref[...]
+    names, rank = ranks_of(tile)
+    hot = jnp.where(names == tile, 1.0, 0.0).astype(BF16)
+    mine = got2[...].reshape(na * nd, LANES)
     none = jnp.zeros((nd, LANES), F32)
     later = jnp.concatenate([mine[nd:], none], axis=0)
     sooner = jnp.concatenate([none, mine[:-nd]], axis=0)
@@ -199,13 +196,10 @@
     for piece in split3(slots):
         term = dot_nn(piece, hot)
         rows = term if rows is None else rows + term
-    total = None
     for k in range(RANKS):
-        term = jnp.where(rank == float(k), rows[8 * k : 8 * k + 8], 0.0)
-        total = term if total is None else total + term
-    out_ref[...] = total
-    for copy in sends:
-        copy.wait_send()
+        part = slice(8 * k, 8 * k + 8)
+        out_ref[part, :] = jnp.where(rank == float(k), rows[part], 0.0)
+    return sends
 
 
 CORNERS = ((-1, -1), (-1, 1), (1, -1), (1, 1))
@@ -216,18 +210,11 @@
 OUTS = BANDS + 6
 
 
-def compute_kernel(
-    side, src_ref, sky_ref, counts_ref, out_ref,
+def compute(
+    side, src_ref, sky_ref, copy_in, out_ref,
     counts, weights, turned, prof_i, prof_j, low_i, low_j, scaled,
-    rim_top, rim_bottom, rim_left, rim_right, sums, count_sem,
+    rim_top, rim_bottom, rim_left, rim_right, sums,
 ):
-    slots = RANKS * LANES
-
-    def copy_in(b):
-        return pltpu.make_async_copy(counts_ref.at[b], counts.at[b], count_sem.at[b])
-
-    for b in range(BANDS):
-        copy_in(b).start()
     index = {group: n for n, group in enumerate(GROUPS)}
 
     def source(group, k, row):
@@ -420,85 +407,87 @@
             out_ref[dc + 1, start + 7 : start + 8, :] = second * square - zeroth
 
 
-def compute_call(side, na, nd, routed, sky_level, counts):
-    slots = RANKS * LANES
-    dma = pltpu.SemaphoreType.DMA
-
-    def extent(step):
-        return EDGE if step else side
-
-    prof_i = [pltpu.VMEM((extent(g[0]), slots), F32) for g in GROUPS]
-    prof_j = [pltpu.VMEM((extent(g[1]), slots), F32) for g in GROUPS]
-    low_i = [pltpu.VMEM((extent(g[0]) if g[0] == 0 else 16, slots), BF16) for g in GROUPS]
-    low_j = [pltpu.VMEM((extent(g[1]) if g[0] or not g[1] else 16, slots), BF16) for g in GROUPS]
-    scaled = [pltpu.VMEM((BANDS * (EDGE if g != (0, 0) else side), slots), BF16) for g in GROUPS]
-    return pl.pallas_call(
-        functools.partial(compute_kernel, side),
-        out_shape=jax.ShapeDtypeStruct((3, LANES, na * nd), F32),
-        in_specs=[
-            VMEM,
-            pl.BlockSpec(memory_space=pltpu.SMEM),
-            pl.BlockSpec(memory_space=pl.ANY),
-        ],
-        out_specs=VMEM,
-        scratch_shapes=[
-            pltpu.VMEM((BANDS, side, side), jnp.int32),
-            pltpu.VMEM((BANDS, side, side), BF16),
-            pltpu.VMEM((side, BANDS * side), BF16),
-            prof_i, prof_j, low_i, low_j, scaled,
-            pltpu.VMEM((BANDS, EDGE, side), F32),
-            pltpu.VMEM((BANDS, EDGE, side), F32),
-            pltpu.VMEM((side, BANDS * EDGE), F32),
-            pltpu.VMEM((side, BANDS * EDGE), F32),
-            pltpu.VMEM((len(GROUPS), RANKS, OUTS, 8, LANES), F32),
-            dma((BANDS,)),
-        ],
-        compiler_params=pltpu.CompilerParams(vmem_limit_bytes=60 << 20),
-        name="compute",
-    )(routed, sky_level, counts)
+def fused_kernel(
+    na, nd, side, flux_ref, pos_ref, width_ref, tile_ref, sky_ref, counts_ref, out_ref,
+    counts, count_sem, sources, partial, to_route, to_compute, to_return,
+):
+    def copy_in(b):
+        return pltpu.make_async_copy(counts_ref.at[b], counts.at[b], count_sem.at[b])
+
+    for b in range(BANDS):
+        copy_in(b).start()
+    sends = route(na, nd, flux_ref, pos_ref, width_ref, tile_ref, sources, *to_route)
+    compute(side, sources, sky_ref, copy_in, partial, counts, *to_compute)
+    sends += give_back(na, nd, partial, tile_ref, out_ref, *to_return)
+    for copy in sends:
+        copy.wait_send()
 
 
 def on_device(na, nd, log_flux, position, log_width, owner_tile, sky_level, counts):
     rows = log_flux.shape[1]
     side = counts.shape[1]
+    slots = RANKS * LANES
     width = log_width.reshape(1, rows)
     tile = owner_tile.reshape(1, rows)
     dma = pltpu.SemaphoreType.DMA
 
-    routed = pl.pallas_call(
-        functools.partial(route_kernel, na, nd),
-        out_shape=jax.ShapeDtypeStruct((3, LANES, na * nd), F32),
-        in_specs=[VMEM] * 4,
+    def extent(step):
+        return EDGE if step else side
+
+    def buffer(*shape, dtype=F32):
+        return pltpu.VMEM(shape, dtype)
+
+    spare = 16
+    masked = pl.pallas_call(
+        functools.partial(fused_kernel, na, nd, side),
+        out_shape=jax.ShapeDtypeStruct((RANKS * 8, rows), F32),
+        in_specs=[VMEM] * 4
+        + [pl.BlockSpec(memory_space=pltpu.SMEM), pl.BlockSpec(memory_space=pl.ANY)],
         out_specs=VMEM,
         scratch_shapes=[
-            pltpu.VMEM((8, rows), F32),
-            pltpu.VMEM((na, nd, LANES), F32),
-            pltpu.VMEM((na, nd, LANES), F32),
-            pltpu.VMEM((nd + 2, na, LANES), F32),
-            pltpu.VMEM((nd, 3, na, LANES), F32),
-            dma((na,)), dma((na,)), dma((nd,)), dma((nd,)),
+            buffer(BANDS, side, side, dtype=jnp.int32),
+            dma((BANDS,)),
+            buffer(3, LANES, na * nd),
+            buffer(3, LANES, na * nd),
+            [
+                buffer(8, rows),
+                buffer(na, nd, LANES),
+                buffer(na, nd, LANES),
+                buffer(nd + 2, na, LANES),
+                buffer(nd, 3, na, LANES),
+                dma((na,)), dma((na,)), dma((nd,)), dma((nd,)),
+            ],
+            [
+                buffer(BANDS, side, side, dtype=BF16),
+                buffer(side, BANDS * side, dtype=BF16),
+                [buffer(extent(g[0]), slots) for g in GROUPS],
+                [buffer(extent(g[1]), slots) for g in GROUPS],
+                [buffer(spare if g[0] else side, slots, dtype=BF16) for g in GROUPS],
+                [
+                    buffer(extent(g[1]) if g[0] or not g[1] else spare, slots, dtype=BF16)
+                    for g in GROUPS
+                ],
+                [buffer(BANDS * (EDGE if any(g) else side), slots, dtype=BF16) for g in GROUPS],
+                buffer(BANDS, EDGE, side),
+                buffer(BANDS, EDGE, side),
+                buffer(side, BANDS * EDGE),
+                buffer(side, BANDS * EDGE),
+                buffer(len(GROUPS), RANKS, OUTS, 8, LANES),
+            ],
+            [
+                buffer(nd, 3, na, LANES),
+                buffer(nd, 3, na, LANES),
+                buffer(na, nd, LANES),
+                buffer(na, nd, LANES),
+                dma((nd,)), dma((nd,)), dma((na,)), dma((na,)),
+            ],
         ],
-        compiler_params=pltpu.CompilerParams(collective_id=0, has_side_effects=True),
-        name="route",
-    )(log_flux, position, width, tile)
-
-    partial = compute_call(side, na, nd, routed, sky_level, counts)
-
-    return pl.pallas_call(
-        functools.partial(return_kernel, na, nd),
-        out_shape=jax.ShapeDtypeStruct((8, rows), F32),
-        in_specs=[VMEM] * 2,
-        out_specs=VMEM,
-        scratch_shapes=[
-            pltpu.VMEM((nd, 3, na, LANES), F32),
-            pltpu.VMEM((nd + 2, 3, na, LANES), F32),
-            pltpu.VMEM((na, nd, LANES), F32),
-            pltpu.VMEM((na + 2, nd, LANES), F32),
-            dma((nd,)), dma((nd,)), dma((na,)), dma((na,)),
-        ],
-        compiler_params=pltpu.CompilerParams(collective_id=1, has_side_effects=True),
-        name="give_back",
-    )(partial, tile)
+        compiler_params=pltpu.CompilerParams(
+            collective_id=0, has_side_effects=True, vmem_limit_bytes=60 << 20
+        ),
+        name="fused",
+    )(log_flux, position, width, tile, sky_level, counts)
+    return jnp.sum(masked.reshape(RANKS, 8, rows), axis=0)
 
 
 def solution(mesh):

time: 59.9 us -> 53.7 us (0.90)
  Pallas kernels: 58.4 us -> 52.1 us
  other arithmetic: 0 us -> 1.36 us
  local copies, waits for them, and re-layouts: 1.3 us -> 0 us
    pallas_call x3 -> x1, Pallas kernels: 58.4 us -> 52.1 us  [on_device(): pl.pallas_call(functools.partial(fused_kernel, na, nd, side), out_shape=j...]
    reduce_sum x0 -> x1, other arithmetic: none -> 1.36 us  [on_device(): return jnp.sum(masked.reshape(RANKS, 8, rows), axis=0)]
    unnamed x1 -> x0, local copies, waits for them, and re-layouts: 1.3 us -> none
where the time goes in v3:
time: 53.7 us; the launch traced here: 53.5 us
  Pallas kernels  52.1 us (97%)
  other arithmetic  1.36 us (3%)
    pallas_call x1, Pallas kernels, on_device(): pl.pallas_call(functools.partial(fused_kernel, na, nd, side), out_shape=j...  52.1 us
    reduce_sum x1, other arithmetic, on_device(): return jnp.sum(masked.reshape(RANKS, 8, rows), axis=0)  1.36 us

profile of v3, /device:TPU:1, one launch (start us, length us, event | category | flops | bytes accessed | tf_op | source)
XLA Modules:
  0.0 53.5 jit_solution(18394447554995972806)
XLA Ops:
  0.0 52.1 %fused.1 = f32[32,256]{1,0:T(8,128)} custom-call(f32[5,256]{1,0:T(8,128)} %flux_ref.1, f32[2,256]{1,0:T(2,128)} %pos_ref.1, f32[1,256]{1,0:T(1,128)} %bitcast.4, s32[1,256]{1,0:T(1,128)} %bitcast.5, f32[1,1,5]{2,1,0:T(1,128)} %sky_ref.1, s32[5,640,640]{2,1,0:T(8,128)} %counts_ref.1), custom_call_target="tpu_custom_call" | custom-call | tf_op jit(solution)/shard_map/fused/pallas_call | solution.py:441
  52.1 1.4 %bitcast_reduce_fusion = f32[8,256]{1,0:T(8,128)} fusion(f32[32,256]{1,0:T(8,128)} %fused.1), kind=kLoop, calls=%fused_computation | loop fusion | flops 6144 | bytes 40960 | tf_op jit(solution)/shard_map/reduce_sum | solution.py:490

commit v4 on v3

v4 whole, which is shorter than its diff:
```python
import functools
import math

import jax
import jax.numpy as jnp
from jax import lax
from jax.experimental import pallas as pl
from jax.experimental.pallas import tpu as pltpu
from jax.sharding import PartitionSpec as P

F32 = jnp.float32
BF16 = jnp.bfloat16
MESH = pl.DeviceIdType.MESH
VMEM = pl.BlockSpec(memory_space=pltpu.VMEM)

EDGE = 128
RANKS = 4
LANES = 128
HALF_LOG2E = 0.5 * math.log2(math.e)
ROOT_2PI = math.sqrt(2.0 * math.pi)


def split3(x):
    hi = x.astype(BF16)
    rest = x - hi.astype(F32)
    mid = rest.astype(BF16)
    lo = (rest - mid.astype(F32)).astype(BF16)
    return hi, mid, lo


def dot_tt(a, b):
    return lax.dot_general(a, b, (((1,), (1,)), ((), ())), preferred_element_type=F32)


def dot_nn(a, b):
    return lax.dot_general(a, b, (((1,), (0,)), ((), ())), preferred_element_type=F32)


def ranks_of(tile):
    rows = tile.shape[1]
    names = lax.broadcasted_iota(jnp.int32, (LANES, rows), 0)
    onehot = names == tile
    earlier = lax.broadcasted_iota(jnp.int32, (rows, rows), 0) < lax.broadcasted_iota(
        jnp.int32, (rows, rows), 1
    )
    before = dot_nn(
        jnp.where(onehot, 1.0, 0.0).astype(BF16), jnp.where(earlier, 1.0, 0.0).astype(BF16)
    )
    rank = jnp.sum(jnp.where(onehot, before, 0.0), axis=0, keepdims=True)
    return names, rank


def far_first(na, nd):
    ring_x, ring_z = na // 4, nd // 2
    along_ra = [(x, y, core) for x in range(ring_x) for y in range(2) for core in range(2)][1:]
    along_ra.sort(key=lambda o: -(4 * min(o[0], ring_x - o[0]) + 8 * o[1] + o[2]))
    along_dec = [(z, y) for z in range(ring_z) for y in range(2)][1:]
    along_dec.sort(key=lambda o: -(2 * min(o[0], ring_z - o[0]) + 2 * o[1]))
    a, d = lax.axis_index("ra"), lax.axis_index("dec")
    ra = [
        lax.rem(a // 4 + x, ring_x) * 4 + lax.rem(a // 2 + y, 2) * 2 + lax.rem(a + core, 2)
        for x, y, core in along_ra
    ]
    dec = [lax.rem(d // 2 + z, ring_z) * 2 + lax.rem(d + y, 2) for z, y in along_dec]
    return a, d, ra, dec


def send(src, dst, send_sem, recv_sem, a, d):
    return pltpu.make_async_remote_copy(
        src_ref=src, dst_ref=dst, send_sem=send_sem, recv_sem=recv_sem,
        device_id=(a, d), device_id_type=MESH,
    )


def greet(peers):
    a, d, ra, dec = peers
    barrier = pltpu.get_barrier_semaphore()
    for peer in ra:
        pl.semaphore_signal(barrier, inc=1, device_id=(peer, d), device_id_type=MESH)
    for peer in dec:
        pl.semaphore_signal(barrier, inc=1, device_id=(a, peer), device_id_type=MESH)


def route(
    na, nd, peers, fetched, out_ref,
    flux, position, width, tiles, params, onehot, ranks, first, got1, stage, got2,
    send1, recv1, send2, recv2,
):
    a, d, ra, dec = peers
    stage[0] = jnp.zeros((na, LANES), F32)
    stage[nd + 1] = jnp.zeros((na, LANES), F32)
    for copy in fetched:
        copy.wait()
    params[0:5, :] = jnp.exp(flux[...])
    params[5:7, :] = position[...]
    params[7:8, :] = width[...]
    tile = tiles[...]
    rows = tile.shape[1]
    names, rank = ranks_of(tile)
    ranks[...] = rank
    onehot[...] = jnp.where(names == tile, 1.0, 0.0).astype(BF16)
    block = params[...]
    ranked = jnp.concatenate(
        [jnp.where(rank == float(k), block, 0.0) for k in range(RANKS)], axis=0
    )
    gap = jnp.zeros((LANES - ranked.shape[0] * 3, rows), BF16)
    none = jnp.zeros(ranked.shape, BF16)
    pieces = split3(ranked)
    total = None
    for n in range(3):
        hot = jnp.where(names + (n - 1) * nd == tile, 1.0, 0.0).astype(BF16)
        for piece in pieces:
            rhs = jnp.concatenate([piece if m == n else none for m in range(3)] + [gap], axis=0)
            term = dot_tt(hot, rhs)
            total = term if total is None else total + term
    first[...] = total.reshape(na, nd, LANES)
    pl.semaphore_wait(pltpu.get_barrier_semaphore(), len(ra) + len(dec))

    sends = []
    for i, peer in enumerate(ra):
        copy = send(first.at[peer], got1.at[a], send1.at[i], recv1.at[a], peer, d)
        copy.start()
        sends.append(copy)
    got1[a] = first[a]
    for i, peer in enumerate(ra):
        send(first.at[peer], got1.at[peer], send1.at[i], recv1.at[peer], peer, d).wait_recv()
    for col in range(nd):
        stage[col + 1] = got1[:, col, :]
    for i, peer in enumerate(dec):
        copy = send(
            stage.at[pl.ds(peer, 3)], got2.at[d], send2.at[i], recv2.at[d], a, peer
        )
        copy.start()
        sends.append(copy)
    got2[d] = stage[pl.ds(d, 3)]
    for i, peer in enumerate(dec):
        send(
            stage.at[pl.ds(peer, 3)], got2.at[peer], send2.at[i], recv2.at[peer], a, peer
        ).wait_recv()
    for n in range(3):
        out_ref[n] = got2[:, n].reshape(na * nd, LANES).T
    return sends


class GiveBack:
    def __init__(self, na, nd, peers, grad_ref, first, got1, stage, got2, send1, recv1, send2, recv2):
        self.na, self.nd, self.peers, self.grad_ref = na, nd, peers, grad_ref
        self.first, self.got1, self.stage, self.got2 = first, got1, stage, got2
        self.send1, self.recv1, self.send2, self.recv2 = send1, recv1, send2, recv2
        self.sends = []

    def along_dec(self, n, i, place):
        a, _, _, dec = self.peers
        return send(
            self.first.at[n, dec[i]], self.got1.at[n, place],
            self.send1.at[n, i], self.recv1.at[n, place], a, dec[i],
        )

    def start(self, n):
        _, d, _, dec = self.peers
        self.first[n] = self.grad_ref[n].T.reshape(self.nd, self.na, LANES)
        for i in range(len(dec)):
            copy = self.along_dec(n, i, d)
            copy.start()
            self.sends.append(copy)
        self.got1[n, d] = self.first[n, d]

    def finish(self, onehot, ranks, out_ref):
        na, nd, got1, stage, got2 = self.na, self.nd, self.got1, self.stage, self.got2
        a, d, ra, dec = self.peers
        for n in (0, 2, 1):
            for i, peer in enumerate(dec):
                self.along_dec(n, i, peer).wait_recv()
        for col in range(nd):
            part = got1[1, col]
            if col + 1 < nd:
                part = part + got1[0, col + 1]
            if col:
                part = part + got1[2, col - 1]
            stage[:, col, :] = part
        for i, peer in enumerate(ra):
            copy = send(stage.at[peer], got2.at[a], self.send2.at[i], self.recv2.at[a], peer, d)
            copy.start()
            self.sends.append(copy)
        got2[a] = stage[a]
        for i, peer in enumerate(ra):
            send(
                stage.at[peer], got2.at[peer], self.send2.at[i], self.recv2.at[peer], peer, d
            ).wait_recv()
        mine = got2[...].reshape(na * nd, LANES)
        none = jnp.zeros((nd, LANES), F32)
        later = jnp.concatenate([mine[nd:], none], axis=0)
        sooner = jnp.concatenate([none, mine[:-nd]], axis=0)
        held, width = mine.T, 8 * RANKS
        slots = (
            later.T[0:width] + held[width : 2 * width] + sooner.T[2 * width : 3 * width]
        )
        rows = None
        for piece in split3(slots):
            term = dot_nn(piece, onehot[...])
            rows = term if rows is None else rows + term
        rank = ranks[...]
        for k in range(RANKS):
            part = slice(8 * k, 8 * k + 8)
            out_ref[part, :] = jnp.where(rank == float(k), rows[part], 0.0)
        for copy in self.sends:
            copy.wait_send()


CORNERS = ((-1, -1), (-1, 1), (1, -1), (1, 1))
SIDES = ((-1, 0), (1, 0), (0, -1), (0, 1))
GROUPS = CORNERS + SIDES + ((0, 0),)
BANDS = 5
STEP = 64
OUTS = BANDS + 6


def compute(
    side, src_ref, sky_ref, copy_in, out_ref, done,
    counts, weights, turned, prof_i, prof_j, low_i, low_j, scaled,
    rim_top, rim_bottom, rim_left, rim_right, sums,
):
    index = {group: n for n, group in enumerate(GROUPS)}

    def source(group, k, row):
        dr, dc = group
        start = (dr + 1) * 8 * RANKS + k * 8 + row
        return src_ref[dc + 1, start : start + 1, :]

    def span(step):
        if step == 0:
            return 0, side
        return (0, EDGE) if step < 0 else (side - EDGE, EDGE)

    def make_profile(group, axis, f32_ref, low_ref, scaled_ref):
        first, count = span(group[axis])
        base = first + 0.5 - group[axis] * side
        iota = lax.broadcasted_iota(jnp.int32, (STEP, LANES), 0).astype(F32)
        for k in range(RANKS):
            lanes = slice(k * LANES, (k + 1) * LANES)
            center = source(group, k, 5 + axis)
            inverse = 1.0 / (float(EDGE) * jnp.exp(source(group, k, 7)))
            factor = -HALF_LOG2E * inverse * inverse
            norm = inverse * (1.0 / ROOT_2PI)
            flux = [source(group, k, b) for b in range(BANDS)] if scaled_ref is not None else []

            def body(step, carry):
                start = pl.multiple_of(step * STEP, STEP)
                off = iota + (base + start.astype(F32)) - center
                prof = jnp.exp2(off * factor * off) * norm
                rows = pl.ds(start, STEP)
                f32_ref[rows, lanes] = prof
                if low_ref is not None:
                    low_ref[rows, lanes] = prof.astype(BF16)
                for b, f in enumerate(flux):
                    into = pl.ds(pl.multiple_of(b * count + step * STEP, STEP), STEP)
                    scaled_ref[into, lanes] = (prof * f).astype(BF16)
                return carry

            lax.fori_loop(0, count // STEP, body, 0, unroll=True)

    def rounded(x):
        return x.astype(BF16).astype(F32)

    class Pipeline:
        def __init__(self):
            self.held = None

        def add(self, product, consume):
            value = product()
            self.flush()
            self.held = functools.partial(consume, value)

        def flush(self):
            if self.held is not None:
                self.held()
            self.held = None

    line = Pipeline()
    rims_ij = {-1: rim_top, 1: rim_bottom}
    rims_ji = {-1: rim_left, 1: rim_right}
    own = index[(0, 0)]

    def profiles(group):
        n = index[group]
        by_row = group[0] or not group[1]
        make_profile(group, 0, prof_i[n], None if group[0] else low_i[n], scaled[n] if by_row else None)
        make_profile(group, 1, prof_j[n], low_j[n] if by_row else None, None if by_row else scaled[n])

    def render(group):
        n = index[group]
        if group[0] or not group[1]:
            return dot_tt(scaled[n][...], low_j[n][...])
        return dot_tt(low_i[n][...], scaled[n][...])

    def add_rim(group, model):
        dr, dc = group
        if dr:
            part = rounded(model).reshape(BANDS, EDGE, model.shape[1])
            if dc == 0:
                rims_ij[dr][...] = part
            else:
                start = 0 if dc < 0 else side - EDGE
                rims_ij[dr][:, :, start : start + EDGE] += part
        else:
            rims_ji[dc][...] = rounded(model)

    around = SIDES + CORNERS
    profiles(around[0])
    for here, following in zip(around, around[1:] + ((0, 0),)):
        profiles(following)
        line.add(functools.partial(render, here), functools.partial(add_rim, here))

    def own_model(b):
        return dot_tt(scaled[own][b * side : (b + 1) * side, :], low_j[own][...])

    def weigh(b, model):
        level = sky_ref[0, 0:1, b : b + 1]
        for chunk in range(side // EDGE):
            rows = slice(chunk * EDGE, (chunk + 1) * EDGE)
            for other in range(side // EDGE):
                cols = slice(other * EDGE, (other + 1) * EDGE)
                part = rounded(model[rows, cols]) + level
                if other == 0:
                    part = part + rim_left[rows, b * EDGE : (b + 1) * EDGE]
                if other == side // EDGE - 1:
                    part = part + rim_right[rows, b * EDGE : (b + 1) * EDGE]
                if chunk == 0:
                    part = part + rim_top[b, :, cols]
                if chunk == side // EDGE - 1:
                    part = part + rim_bottom[b, :, cols]
                ratio = counts[b, rows, cols].astype(F32) / part - 1.0
                low = ratio.astype(BF16)
                weights[b, rows, cols] = low
                turned[cols, b * side + chunk * EDGE : b * side + (chunk + 1) * EDGE] = low.T

    for b in range(BANDS):
        copy_in(b).wait()
    for b in range(BANDS):
        line.add(functools.partial(own_model, b), functools.partial(weigh, b))
    line.flush()

    def fold(x):
        return jnp.sum(x.reshape(x.shape[0] // 8, 8, x.shape[1]), axis=0)

    def put(n, k, at, value, add):
        if add:
            sums[n, k, at] += value
        else:
            sums[n, k, at] = value

    def moments(group, axis, k, start, total, prof, base, add):
        n = index[group]
        iota = lax.broadcasted_iota(jnp.int32, (8, LANES), 0).astype(F32)
        zeroth = first = second = None
        for run in range(total.shape[0] // EDGE):
            s0 = s1 = s2 = None
            for row in range(run * EDGE, (run + 1) * EDGE, 8):
                term = prof[row : row + 8] * total[row : row + 8]
                s0 = term if s0 is None else s0 + term
                s1 = s0 if s1 is None else s1 + s0
                s2 = s1 if s2 is None else s2 + s1
            end = iota + (base + (start + (run + 1) * EDGE)) - source(group, k, 5 + axis)
            scaled0 = end * s0
            one = scaled0 - 8.0 * s1
            two = end * (scaled0 - 16.0 * s1) + 64.0 * (s2 + (s2 - s1))
            zeroth = s0 if zeroth is None else zeroth + s0
            first = one if first is None else first + one
            second = two if second is None else second + two
        at = BANDS + 3 * axis
        put(n, k, at, zeroth, add)
        put(n, k, at + 1, first, add)
        put(n, k, at + 2, second, add)

    def per_band(group, axis, lhs, rhs, prof_ref, start, add):
        n = index[group]
        base = span(group[axis])[0] + 0.5 - group[axis] * side

        def consume(pair, along):
            for k in (2 * pair, 2 * pair + 1):
                lanes = slice((k - 2 * pair) * LANES, (k - 2 * pair + 1) * LANES)
                prof = prof_ref[start : start + EDGE, k * LANES : (k + 1) * LANES]
                low = rounded(prof)
                total = None
                for b in range(BANDS):
                    band = along[b * EDGE : (b + 1) * EDGE, lanes]
                    put(n, k, b, fold(low * band), add)
                    term = source(group, k, b) * band
                    total = term if total is None else total + term
                moments(group, axis, k, start, total, prof, base, add)

        for pair in range(RANKS // 2):
            wide = slice(pair * 2 * LANES, (pair + 1) * 2 * LANES)
            line.add(
                lambda wide=wide: dot_nn(lhs(), rhs[:, wide]), functools.partial(consume, pair)
            )

    def all_bands(group, axis, lhs, scaled_ref, prof_ref):
        base = span(group[axis])[0] + 0.5 - group[axis] * side

        def consume(pair, along):
            for k in (2 * pair, 2 * pair + 1):
                lanes = slice((k - 2 * pair) * LANES, (k - 2 * pair + 1) * LANES)
                prof = prof_ref[:, k * LANES : (k + 1) * LANES]
                moments(group, axis, k, 0, along[:, lanes], prof, base, False)

        for pair in range(RANKS // 2):
            wide = slice(pair * 2 * LANES, (pair + 1) * 2 * LANES)
            line.add(
                lambda wide=wide: dot_nn(lhs(), scaled_ref[:, wide]),
                functools.partial(consume, pair),
            )

    def near_rows(group):
        (r0, rn), (c0, cn) = span(group[0]), span(group[1])
        return weights[:, r0 : r0 + rn, c0 : c0 + cn].reshape(BANDS * rn, cn)

    def far_cols(group):
        (r0, rn), (c0, cn) = span(group[0]), span(group[1])
        at = [b * side + r0 for b in range(BANDS)]
        return jnp.concatenate([turned[c0 : c0 + cn, r : r + rn] for r in at], axis=1)

    def near_cols(group):
        c0, cn = span(group[1])
        at = [b * side for b in range(BANDS)]
        return jnp.concatenate([turned[c0 : c0 + cn, r : r + side] for r in at], axis=0)

    def far_rows(group):
        c0, cn = span(group[1])
        return jnp.concatenate([weights[b, :, c0 : c0 + cn] for b in range(BANDS)], axis=1)

    def side_grads(group):
        n = index[group]
        if group[0]:
            lhs = functools.partial(near_rows, group)
            per_band(group, 0, lhs, low_j[n], prof_i[n], 0, False)
            all_bands(group, 1, functools.partial(far_cols, group), scaled[n], prof_j[n])
        else:
            lhs = functools.partial(near_cols, group)
            per_band(group, 1, lhs, low_i[n], prof_j[n], 0, False)
            all_bands(group, 0, functools.partial(far_rows, group), scaled[n], prof_i[n])

    def own_rows(start):
        return weights[:, start : start + EDGE, :].reshape(BANDS * EDGE, side)

    def own_grads():
        for start in range(0, side, EDGE):
            lhs = functools.partial(own_rows, start)
            per_band((0, 0), 0, lhs, low_j[own], prof_i[own], start, start > 0)
        all_bands((0, 0), 1, lambda: turned[...], scaled[own], prof_j[own])

    def collect(group):
        n, (dr, dc) = index[group], group
        for k in range(RANKS):
            inverse = 1.0 / (float(EDGE) * jnp.exp(source(group, k, 7)))
            square = inverse * inverse

            def total(which):
                return jnp.sum(sums[n, k, which], axis=0, keepdims=True)

            start = (dr + 1) * 8 * RANKS + k * 8
            for b in range(BANDS):
                out_ref[dc + 1, start + b : start + b + 1, :] = source(group, k, b) * total(b)
            zeroth = total(BANDS) + total(BANDS + 3)
            second = total(BANDS + 2) + total(BANDS + 5)
            out_ref[dc + 1, start + 5 : start + 6, :] = total(BANDS + 1) * square
            out_ref[dc + 1, start + 6 : start + 7, :] = total(BANDS + 4) * square
            out_ref[dc + 1, start + 7 : start + 8, :] = second * square - zeroth

    for step in (-1, 1, 0):
        groups = [group for group in around if group[1] == step]
        for group in groups:
            side_grads(group)
        if step == 0:
            own_grads()
            groups.append((0, 0))
        line.flush()
        out_ref[step + 1] = jnp.zeros(out_ref.shape[1:], F32)
        for group in groups:
            collect(group)
        done(step + 1)


def fused_kernel(
    na, nd, side, flux_ref, pos_ref, width_ref, tile_ref, sky_ref, counts_ref, out_ref,
    counts, count_sem, sky, flux, position, width, tiles, input_sem, onehot, ranks,
    sources, partial, to_route, to_compute, to_return,
):
    peers = far_first(na, nd)
    greet(peers)
    fetched = [
        pltpu.make_async_copy(src, dst, input_sem.at[n])
        for n, (src, dst) in enumerate(
            [
                (tile_ref, tiles), (flux_ref, flux), (pos_ref, position),
                (width_ref, width), (sky_ref, sky),
            ]
        )
    ]
    for copy in fetched:
        copy.start()

    def copy_in(b):
        return pltpu.make_async_copy(counts_ref.at[b], counts.at[b], count_sem.at[b])

    for b in range(BANDS):
        copy_in(b).start()
    params, *rest = to_route
    sends = route(
        na, nd, peers, fetched, sources, flux, position, width, tiles, params, onehot, ranks, *rest
    )
    back = GiveBack(na, nd, peers, partial, *to_return)
    compute(side, sources, sky, copy_in, partial, back.start, counts, *to_compute)
    back.finish(onehot, ranks, out_ref)
    for copy in sends:
        copy.wait_send()


def buffer(*shape, dtype=F32):
    return pltpu.VMEM(shape, dtype)


def compute_buffers(side):
    slots = RANKS * LANES
    spare = 16

    def extent(step):
        return EDGE if step else side

    return [
        buffer(BANDS, side, side, dtype=BF16),
        buffer(side, BANDS * side, dtype=BF16),
        [buffer(extent(g[0]), slots) for g in GROUPS],
        [buffer(extent(g[1]), slots) for g in GROUPS],
        [buffer(spare if g[0] else side, slots, dtype=BF16) for g in GROUPS],
        [
            buffer(extent(g[1]) if g[0] or not g[1] else spare, slots, dtype=BF16)
            for g in GROUPS
        ],
        [buffer(BANDS * (EDGE if any(g) else side), slots, dtype=BF16) for g in GROUPS],
        buffer(BANDS, EDGE, side),
        buffer(BANDS, EDGE, side),
        buffer(side, BANDS * EDGE),
        buffer(side, BANDS * EDGE),
        buffer(len(GROUPS), RANKS, OUTS, 8, LANES),
    ]


def on_device(na, nd, log_flux, position, log_width, owner_tile, sky_level, counts):
    rows = log_flux.shape[1]
    side = counts.shape[1]
    width = log_width.reshape(1, rows)
    tile = owner_tile.reshape(1, rows)
    dma = pltpu.SemaphoreType.DMA

    masked = pl.pallas_call(
        functools.partial(fused_kernel, na, nd, side),
        out_shape=jax.ShapeDtypeStruct((RANKS * 8, rows), F32),
        in_specs=[pl.BlockSpec(memory_space=pl.ANY)] * 6,
        out_specs=VMEM,
        scratch_shapes=[
            buffer(BANDS, side, side, dtype=jnp.int32),
            dma((BANDS,)),
            buffer(*sky_level.shape),
            buffer(*log_flux.shape),
            buffer(*position.shape),
            buffer(1, rows),
            buffer(1, rows, dtype=jnp.int32),
            dma((5,)),
            buffer(LANES, rows, dtype=BF16),
            buffer(1, rows),
            buffer(3, LANES, na * nd),
            buffer(3, LANES, na * nd),
            [
                buffer(8, rows),
                buffer(na, nd, LANES),
                buffer(na, nd, LANES),
                buffer(nd + 2, na, LANES),
                buffer(nd, 3, na, LANES),
                dma((na,)), dma((na,)), dma((nd,)), dma((nd,)),
            ],
            compute_buffers(side),
            [
                buffer(3, nd, na, LANES),
                buffer(3, nd, na, LANES),
                buffer(na, nd, LANES),
                buffer(na, nd, LANES),
                dma((3, nd)), dma((3, nd)), dma((na,)), dma((na,)),
            ],
        ],
        compiler_params=pltpu.CompilerParams(
            collective_id=0, has_side_effects=True, vmem_limit_bytes=60 << 20
        ),
        name="fused",
    )(log_flux, position, width, tile, sky_level, counts)
    return jnp.sum(masked.reshape(RANKS, 8, rows), axis=0)


def solution(mesh):
    na, nd = mesh.shape["ra"], mesh.shape["dec"]
    in_specs = (
        P(None, ("ra", "dec")),
        P(None, ("ra", "dec")),
        P(("ra", "dec")),
        P(("ra", "dec"), None),
        P("ra", "dec", None),
        P(None, "ra", "dec"),
    )
    return jax.shard_map(
        functools.partial(on_device, na, nd),
        mesh=mesh,
        in_specs=in_specs,
        out_specs=P(None, ("ra", "dec")),
        check_vma=False,
    )
```

time: 53.7 us -> 50.8 us (0.946)
  Pallas kernels: 52.1 us -> 49.2 us
    pallas_call x1, Pallas kernels: 52.1 us -> 49.2 us  [on_device(): pl.pallas_call(functools.partial(fused_kernel, na, nd, side), out_shape=j...]
where the time goes in v4:
time: 50.8 us; the launch traced here: 50.6 us
  Pallas kernels  49.2 us (97%)
  other arithmetic  1.36 us (3%)
    pallas_call x1, Pallas kernels, on_device(): pl.pallas_call(functools.partial(fused_kernel, na, nd, side), out_shape=j...  49.2 us
    reduce_sum x1, other arithmetic, on_device(): return jnp.sum(masked.reshape(RANKS, 8, rows), axis=0)  1.36 us

profile of v4, /device:TPU:1, one launch (start us, length us, event | category | flops | bytes accessed | tf_op | source)
XLA Modules:
  0.0 50.6 jit_solution(2239806113382746149)
XLA Ops:
  0.0 49.2 %fused.1 = f32[32,256]{1,0:T(8,128)} custom-call(f32[5,256]{1,0:T(8,128)} %flux_ref.1, f32[2,256]{1,0:T(2,128)} %pos_ref.1, f32[1,256]{1,0:T(1,128)} %bitcast.4, s32[1,256]{1,0:T(1,128)} %bitcast.5, f32[1,1,5]{2,1,0:T(1,128)} %sky_ref.1, s32[5,640,640]{2,1,0:T(8,128)} %counts_ref.1), custom_call_target="tpu_custom_call" | custom-call | tf_op jit(solution)/shard_map/fused/pallas_call | solution.py:556
  49.2 1.4 %bitcast_reduce_fusion = f32[8,256]{1,0:T(8,128)} fusion(f32[32,256]{1,0:T(8,128)} %fused.1), kind=kLoop, calls=%fused_computation | loop fusion | flops 6144 | bytes 40960 | tf_op jit(solution)/shard_map/reduce_sum | solution.py:596

commit v5 on v4

--- a/solution.py
+++ b/solution.py
@@ -50,19 +50,39 @@
     return names, rank
 
 
-def far_first(na, nd):
-    ring_x, ring_z = na // 4, nd // 2
-    along_ra = [(x, y, core) for x in range(ring_x) for y in range(2) for core in range(2)][1:]
-    along_ra.sort(key=lambda o: -(4 * min(o[0], ring_x - o[0]) + 8 * o[1] + o[2]))
-    along_dec = [(z, y) for z in range(ring_z) for y in range(2)][1:]
-    along_dec.sort(key=lambda o: -(2 * min(o[0], ring_z - o[0]) + 2 * o[1]))
-    a, d = lax.axis_index("ra"), lax.axis_index("dec")
-    ra = [
-        lax.rem(a // 4 + x, ring_x) * 4 + lax.rem(a // 2 + y, 2) * 2 + lax.rem(a + core, 2)
-        for x, y, core in along_ra
-    ]
-    dec = [lax.rem(d // 2 + z, ring_z) * 2 + lax.rem(d + y, 2) for z, y in along_dec]
-    return a, d, ra, dec
+class Place:
+    def __init__(self, na, nd):
+        ring_x, ring_z = na // 4, nd // 2
+        a, d = lax.axis_index("ra"), lax.axis_index("dec")
+        x, h, k, z, low = a // 4, lax.rem(a // 2, 2), lax.rem(a, 2), d // 2, lax.rem(d, 2)
+        self.far_count, self.near_count, self.ring_z = ring_x * ring_z, 8, ring_z
+        self.low, self.far_here, self.near_here = low, x * ring_z + z, h * 4 + k * 2 + low
+        steps = [(i, j) for i in range(ring_x) for j in range(ring_z)][1:]
+        steps.sort(key=lambda o: -(min(o[0], ring_x - o[0]) + min(o[1], ring_z - o[1])))
+        self.far = []
+        for i, j in steps:
+            px, pz = lax.rem(x + i, ring_x), lax.rem(z + j, ring_z)
+            self.far.append((px * 4 + h * 2 + k, pz * 2 + low, px * ring_z + pz))
+        turns = [(i, j, m) for i in range(2) for j in range(2) for m in range(2)][1:]
+        turns.sort(key=lambda o: -(4 * o[0] - 2 * o[0] * o[2] + 2 * o[2] + o[1]))
+        self.near = []
+        for i, j, m in turns:
+            ph, pk, pl_ = lax.rem(h + i, 2), lax.rem(k + j, 2), lax.rem(low + m, 2)
+            self.near.append((x * 4 + ph * 2 + pk, z * 2 + pl_, ph * 4 + pk * 2 + pl_))
+
+
+REACH = 6
+SIDE_REACH = 4
+
+
+def reached(na, nd, ring_z, column, rows):
+    number = lax.broadcasted_iota(jnp.int32, (LANES, rows), 0)
+    bits = ring_z.bit_length() - 1
+    step = number & 7
+    a = lax.shift_right_logical(number, 3 + bits) * 4 - 1 + step
+    d = (lax.shift_right_logical(number, 3) & (ring_z - 1)) * 2 - 1 + column
+    known = (step < REACH) & (a >= 0) & (a < na) & (d >= 0) & (d < nd)
+    return jnp.where(known, a * nd + d, -1)
 
 
 def send(src, dst, send_sem, recv_sem, a, d):
@@ -72,23 +92,17 @@
     )
 
 
-def greet(peers):
-    a, d, ra, dec = peers
+def greet(place):
     barrier = pltpu.get_barrier_semaphore()
-    for peer in ra:
-        pl.semaphore_signal(barrier, inc=1, device_id=(peer, d), device_id_type=MESH)
-    for peer in dec:
-        pl.semaphore_signal(barrier, inc=1, device_id=(a, peer), device_id_type=MESH)
+    for a, d, _ in place.far + place.near:
+        pl.semaphore_signal(barrier, inc=1, device_id=(a, d), device_id_type=MESH)
 
 
 def route(
-    na, nd, peers, fetched, out_ref,
+    na, nd, place, fetched, out_ref,
     flux, position, width, tiles, params, onehot, ranks, first, got1, stage, got2,
     send1, recv1, send2, recv2,
 ):
-    a, d, ra, dec = peers
-    stage[0] = jnp.zeros((na, LANES), F32)
-    stage[nd + 1] = jnp.zeros((na, LANES), F32)
     for copy in fetched:
         copy.wait()
     params[0:5, :] = jnp.exp(flux[...])
@@ -96,109 +110,108 @@
     params[7:8, :] = width[...]
     tile = tiles[...]
     rows = tile.shape[1]
-    names, rank = ranks_of(tile)
+    _, rank = ranks_of(tile)
     ranks[...] = rank
-    onehot[...] = jnp.where(names == tile, 1.0, 0.0).astype(BF16)
     block = params[...]
     ranked = jnp.concatenate(
         [jnp.where(rank == float(k), block, 0.0) for k in range(RANKS)], axis=0
     )
-    gap = jnp.zeros((LANES - ranked.shape[0] * 3, rows), BF16)
     none = jnp.zeros(ranked.shape, BF16)
     pieces = split3(ranked)
     total = None
-    for n in range(3):
-        hot = jnp.where(names + (n - 1) * nd == tile, 1.0, 0.0).astype(BF16)
+    for n in range(SIDE_REACH):
+        names = reached(na, nd, place.ring_z, n, rows)
+        hot = jnp.where(names == tile, 1.0, 0.0).astype(BF16)
+        onehot[n] = hot
         for piece in pieces:
-            rhs = jnp.concatenate([piece if m == n else none for m in range(3)] + [gap], axis=0)
+            rhs = jnp.concatenate([piece if m == n else none for m in range(SIDE_REACH)], axis=0)
             term = dot_tt(hot, rhs)
             total = term if total is None else total + term
-    first[...] = total.reshape(na, nd, LANES)
-    pl.semaphore_wait(pltpu.get_barrier_semaphore(), len(ra) + len(dec))
+    first[...] = total.reshape(first.shape)
+    pl.semaphore_wait(pltpu.get_barrier_semaphore(), len(place.far) + len(place.near))
 
     sends = []
-    for i, peer in enumerate(ra):
-        copy = send(first.at[peer], got1.at[a], send1.at[i], recv1.at[a], peer, d)
+    here = place.far_here
+    for i, (a, d, peer) in enumerate(place.far):
+        copy = send(first.at[peer], got1.at[here], send1.at[i], recv1.at[here], a, d)
         copy.start()
         sends.append(copy)
-    got1[a] = first[a]
-    for i, peer in enumerate(ra):
-        send(first.at[peer], got1.at[peer], send1.at[i], recv1.at[peer], peer, d).wait_recv()
-    for col in range(nd):
-        stage[col + 1] = got1[:, col, :]
-    for i, peer in enumerate(dec):
-        copy = send(
-            stage.at[pl.ds(peer, 3)], got2.at[d], send2.at[i], recv2.at[d], a, peer
-        )
+    got1[here] = first[here]
+    for i, (a, d, peer) in enumerate(place.far):
+        send(first.at[peer], got1.at[peer], send1.at[i], recv1.at[peer], a, d).wait_recv()
+    for step in range(REACH):
+        stage[step] = got1[:, step, :]
+    here = place.near_here
+    for i, (a, d, peer) in enumerate(place.near):
+        part = stage.at[pl.ds(peer // 2, 3)]
+        copy = send(part, got2.at[here], send2.at[i], recv2.at[here], a, d)
         copy.start()
         sends.append(copy)
-    got2[d] = stage[pl.ds(d, 3)]
-    for i, peer in enumerate(dec):
-        send(
-            stage.at[pl.ds(peer, 3)], got2.at[peer], send2.at[i], recv2.at[peer], a, peer
-        ).wait_recv()
+    got2[here] = stage[pl.ds(here // 2, 3)]
+    for i, (a, d, peer) in enumerate(place.near):
+        part = stage.at[pl.ds(peer // 2, 3)]
+        send(part, got2.at[peer], send2.at[i], recv2.at[peer], a, d).wait_recv()
     for n in range(3):
-        out_ref[n] = got2[:, n].reshape(na * nd, LANES).T
+        turned = got2[:, n].reshape(LANES, LANES).T
+        out_ref[n] = jnp.where(place.low == 1, pltpu.roll(turned, LANES - 8 * RANKS, 0), turned)
     return sends
 
 
 class GiveBack:
-    def __init__(self, na, nd, peers, grad_ref, first, got1, stage, got2, send1, recv1, send2, recv2):
-        self.na, self.nd, self.peers, self.grad_ref = na, nd, peers, grad_ref
+    def __init__(self, place, grad_ref, first, got1, stage, got2, send1, recv1, send2, recv2):
+        self.place, self.grad_ref = place, grad_ref
         self.first, self.got1, self.stage, self.got2 = first, got1, stage, got2
         self.send1, self.recv1, self.send2, self.recv2 = send1, recv1, send2, recv2
         self.sends = []
-
-    def along_dec(self, n, i, place):
-        a, _, _, dec = self.peers
+        stage[...] = jnp.zeros_like(stage)
+
+    def to_near(self, n, i, number):
+        a, d, peer = self.place.near[i]
         return send(
-            self.first.at[n, dec[i]], self.got1.at[n, place],
-            self.send1.at[n, i], self.recv1.at[n, place], a, dec[i],
+            self.first.at[n, peer], self.got1.at[n, number],
+            self.send1.at[n, i], self.recv1.at[n, number], a, d,
         )
 
     def start(self, n):
-        _, d, _, dec = self.peers
-        self.first[n] = self.grad_ref[n].T.reshape(self.nd, self.na, LANES)
-        for i in range(len(dec)):
-            copy = self.along_dec(n, i, d)
+        place, grads = self.place, self.grad_ref[n]
+        grads = jnp.where(place.low == 1, pltpu.roll(grads, 8 * RANKS, 0), grads)
+        self.first[n] = grads.T.reshape(self.first.shape[1:])
+        for i in range(len(place.near)):
+            copy = self.to_near(n, i, place.near_here)
             copy.start()
             self.sends.append(copy)
-        self.got1[n, d] = self.first[n, d]
+        self.got1[n, place.near_here] = self.first[n, place.near_here]
 
     def finish(self, onehot, ranks, out_ref):
-        na, nd, got1, stage, got2 = self.na, self.nd, self.got1, self.stage, self.got2
-        a, d, ra, dec = self.peers
+        place, got1, stage, got2 = self.place, self.got1, self.stage, self.got2
         for n in (0, 2, 1):
-            for i, peer in enumerate(dec):
-                self.along_dec(n, i, peer).wait_recv()
-        for col in range(nd):
-            part = got1[1, col]
-            if col + 1 < nd:
-                part = part + got1[0, col + 1]
-            if col:
-                part = part + got1[2, col - 1]
-            stage[:, col, :] = part
-        for i, peer in enumerate(ra):
-            copy = send(stage.at[peer], got2.at[a], self.send2.at[i], self.recv2.at[a], peer, d)
+            for i, (_, _, peer) in enumerate(place.near):
+                self.to_near(n, i, peer).wait_recv()
+        for step in range(REACH):
+            part = None
+            for n in range(3):
+                for number in range(place.near_count):
+                    if number // 2 + n == step:
+                        part = got1[n, number] if part is None else part + got1[n, number]
+            stage[:, step, :] = part
+        here = place.far_here
+        for i, (a, d, peer) in enumerate(place.far):
+            copy = send(
+                stage.at[peer], got2.at[here], self.send2.at[i], self.recv2.at[here], a, d
+            )
             copy.start()
             self.sends.append(copy)
-        got2[a] = stage[a]
-        for i, peer in enumerate(ra):
+        got2[here] = stage[here]
+        for i, (a, d, peer) in enumerate(place.far):
             send(
-                stage.at[peer], got2.at[peer], self.send2.at[i], self.recv2.at[peer], peer, d
+                stage.at[peer], got2.at[peer], self.send2.at[i], self.recv2.at[peer], a, d
             ).wait_recv()
-        mine = got2[...].reshape(na * nd, LANES)
-        none = jnp.zeros((nd, LANES), F32)
-        later = jnp.concatenate([mine[nd:], none], axis=0)
-        sooner = jnp.concatenate([none, mine[:-nd]], axis=0)
-        held, width = mine.T, 8 * RANKS
-        slots = (
-            later.T[0:width] + held[width : 2 * width] + sooner.T[2 * width : 3 * width]
-        )
+        held, width = got2[...].reshape(LANES, LANES).T, 8 * RANKS
         rows = None
-        for piece in split3(slots):
-            term = dot_nn(piece, onehot[...])
-            rows = term if rows is None else rows + term
+        for n in range(SIDE_REACH):
+            for piece in split3(held[n * width : (n + 1) * width]):
+                term = dot_nn(piece, onehot[n])
+                rows = term if rows is None else rows + term
         rank = ranks[...]
         for k in range(RANKS):
             part = slice(8 * k, 8 * k + 8)
@@ -224,8 +237,8 @@
 
     def source(group, k, row):
         dr, dc = group
-        start = (dr + 1) * 8 * RANKS + k * 8 + row
-        return src_ref[dc + 1, start : start + 1, :]
+        start = (dc + 1) * 8 * RANKS + k * 8 + row
+        return src_ref[dr + 1, start : start + 1, :]
 
     def span(step):
         if step == 0:
@@ -458,17 +471,17 @@
             def total(which):
                 return jnp.sum(sums[n, k, which], axis=0, keepdims=True)
 
-            start = (dr + 1) * 8 * RANKS + k * 8
+            start = (dc + 1) * 8 * RANKS + k * 8
             for b in range(BANDS):
-                out_ref[dc + 1, start + b : start + b + 1, :] = source(group, k, b) * total(b)
+                out_ref[dr + 1, start + b : start + b + 1, :] = source(group, k, b) * total(b)
             zeroth = total(BANDS) + total(BANDS + 3)
             second = total(BANDS + 2) + total(BANDS + 5)
-            out_ref[dc + 1, start + 5 : start + 6, :] = total(BANDS + 1) * square
-            out_ref[dc + 1, start + 6 : start + 7, :] = total(BANDS + 4) * square
-            out_ref[dc + 1, start + 7 : start + 8, :] = second * square - zeroth
+            out_ref[dr + 1, start + 5 : start + 6, :] = total(BANDS + 1) * square
+            out_ref[dr + 1, start + 6 : start + 7, :] = total(BANDS + 4) * square
+            out_ref[dr + 1, start + 7 : start + 8, :] = second * square - zeroth
 
     for step in (-1, 1, 0):
-        groups = [group for group in around if group[1] == step]
+        groups = [group for group in around if group[0] == step]
         for group in groups:
             side_grads(group)
         if step == 0:
@@ -486,8 +499,8 @@
     counts, count_sem, sky, flux, position, width, tiles, input_sem, onehot, ranks,
     sources, partial, to_route, to_compute, to_return,
 ):
-    peers = far_first(na, nd)
-    greet(peers)
+    place = Place(na, nd)
+    greet(place)
     fetched = [
         pltpu.make_async_copy(src, dst, input_sem.at[n])
         for n, (src, dst) in enumerate(
@@ -507,9 +520,9 @@
         copy_in(b).start()
     params, *rest = to_route
     sends = route(
-        na, nd, peers, fetched, sources, flux, position, width, tiles, params, onehot, ranks, *rest
+        na, nd, place, fetched, sources, flux, position, width, tiles, params, onehot, ranks, *rest
     )
-    back = GiveBack(na, nd, peers, partial, *to_return)
+    back = GiveBack(place, partial, *to_return)
     compute(side, sources, sky, copy_in, partial, back.start, counts, *to_compute)
     back.finish(onehot, ranks, out_ref)
     for copy in sends:
@@ -552,6 +565,8 @@
     width = log_width.reshape(1, rows)
     tile = owner_tile.reshape(1, rows)
     dma = pltpu.SemaphoreType.DMA
+    near = 8
+    far = na * nd // near
 
     masked = pl.pallas_call(
         functools.partial(fused_kernel, na, nd, side),
@@ -567,25 +582,25 @@
             buffer(1, rows),
             buffer(1, rows, dtype=jnp.int32),
             dma((5,)),
-            buffer(LANES, rows, dtype=BF16),
+            buffer(SIDE_REACH, LANES, rows, dtype=BF16),
             buffer(1, rows),
             buffer(3, LANES, na * nd),
             buffer(3, LANES, na * nd),
             [
                 buffer(8, rows),
-                buffer(na, nd, LANES),
-                buffer(na, nd, LANES),
-                buffer(nd + 2, na, LANES),
-                buffer(nd, 3, na, LANES),
-                dma((na,)), dma((na,)), dma((nd,)), dma((nd,)),
+                buffer(far, 8, LANES),
+                buffer(far, 8, LANES),
+                buffer(REACH, far, LANES),
+                buffer(near, 3, far, LANES),
+                dma((far,)), dma((far,)), dma((near,)), dma((near,)),
             ],
             compute_buffers(side),
             [
-                buffer(3, nd, na, LANES),
-                buffer(3, nd, na, LANES),
-                buffer(na, nd, LANES),
-                buffer(na, nd, LANES),
-                dma((3, nd)), dma((3, nd)), dma((na,)), dma((na,)),
+                buffer(3, near, far, LANES),
+                buffer(3, near, far, LANES),
+                buffer(far, 8, LANES),
+                buffer(far, 8, LANES),
+                dma((3, near)), dma((3, near)), dma((far,)), dma((far,)),
             ],
         ],
         compiler_params=pltpu.CompilerParams(

time: 50.8 us -> 49.1 us (0.967)
  Pallas kernels: 49.2 us -> 47.4 us
    pallas_call x1, Pallas kernels: 49.2 us -> 47.4 us  [on_device(): pl.pallas_call(functools.partial(fused_kernel, na, nd, side), out_shape=j...]
where the time goes in v5:
time: 49.1 us; the launch traced here: 48.7 us
  Pallas kernels  47.4 us (97%)
  other arithmetic  1.36 us (3%)
    pallas_call x1, Pallas kernels, on_device(): pl.pallas_call(functools.partial(fused_kernel, na, nd, side), out_shape=j...  47.4 us
    reduce_sum x1, other arithmetic, on_device(): return jnp.sum(masked.reshape(RANKS, 8, rows), axis=0)  1.36 us

profile of v5, /device:TPU:1, one launch (start us, length us, event | category | flops | bytes accessed | tf_op | source)
XLA Modules:
  0.0 48.7 jit_solution(12286512045255735624)
XLA Ops:
  0.0 47.4 %fused.1 = f32[32,256]{1,0:T(8,128)} custom-call(f32[5,256]{1,0:T(8,128)} %flux_ref.1, f32[2,256]{1,0:T(2,128)} %pos_ref.1, f32[1,256]{1,0:T(1,128)} %bitcast.4, s32[1,256]{1,0:T(1,128)} %bitcast.5, f32[1,1,5]{2,1,0:T(1,128)} %sky_ref.1, s32[5,640,640]{2,1,0:T(8,128)} %counts_ref.1), custom_call_target="tpu_custom_call" | custom-call | tf_op jit(solution)/shard_map/fused/pallas_call | solution.py:571
  47.4 1.4 %bitcast_reduce_fusion = f32[8,256]{1,0:T(8,128)} fusion(f32[32,256]{1,0:T(8,128)} %fused.1), kind=kLoop, calls=%fused_computation | loop fusion | flops 6144 | bytes 40960 | tf_op jit(solution)/shard_map/reduce_sum | solution.py:611

commit v6 on v5

--- a/solution.py
+++ b/solution.py
@@ -165,34 +165,31 @@
         self.sends = []
         stage[...] = jnp.zeros_like(stage)
 
-    def to_near(self, n, i, number):
+    def to_near(self, i, number):
         a, d, peer = self.place.near[i]
         return send(
-            self.first.at[n, peer], self.got1.at[n, number],
-            self.send1.at[n, i], self.recv1.at[n, number], a, d,
+            self.first.at[peer], self.got1.at[number], self.send1.at[i], self.recv1.at[number], a, d
         )
 
-    def start(self, n):
-        place, grads = self.place, self.grad_ref[n]
-        grads = jnp.where(place.low == 1, pltpu.roll(grads, 8 * RANKS, 0), grads)
-        self.first[n] = grads.T.reshape(self.first.shape[1:])
+    def finish(self, onehot, ranks, out_ref):
+        place, got1, stage, got2 = self.place, self.got1, self.stage, self.got2
+        for n in range(3):
+            grads = self.grad_ref[n]
+            grads = jnp.where(place.low == 1, pltpu.roll(grads, 8 * RANKS, 0), grads)
+            self.first[:, n] = grads.T.reshape(place.near_count, place.far_count, LANES)
         for i in range(len(place.near)):
-            copy = self.to_near(n, i, place.near_here)
+            copy = self.to_near(i, place.near_here)
             copy.start()
             self.sends.append(copy)
-        self.got1[n, place.near_here] = self.first[n, place.near_here]
-
-    def finish(self, onehot, ranks, out_ref):
-        place, got1, stage, got2 = self.place, self.got1, self.stage, self.got2
-        for n in (0, 2, 1):
-            for i, (_, _, peer) in enumerate(place.near):
-                self.to_near(n, i, peer).wait_recv()
+        got1[place.near_here] = self.first[place.near_here]
+        for i, (_, _, peer) in enumerate(place.near):
+            self.to_near(i, peer).wait_recv()
         for step in range(REACH):
             part = None
             for n in range(3):
                 for number in range(place.near_count):
                     if number // 2 + n == step:
-                        part = got1[n, number] if part is None else part + got1[n, number]
+                        part = got1[number, n] if part is None else part + got1[number, n]
             stage[:, step, :] = part
         here = place.far_here
         for i, (a, d, peer) in enumerate(place.far):
@@ -229,10 +226,12 @@
 
 
 def compute(
-    side, src_ref, sky_ref, copy_in, out_ref, done,
+    side, src_ref, sky_ref, copy_in, out_ref,
     counts, weights, turned, prof_i, prof_j, low_i, low_j, scaled,
     rim_top, rim_bottom, rim_left, rim_right, sums,
 ):
+    for b in range(BANDS):
+        copy_in(b).wait()
     index = {group: n for n, group in enumerate(GROUPS)}
 
     def source(group, k, row):
@@ -347,8 +346,6 @@
                 weights[b, rows, cols] = low
                 turned[cols, b * side + chunk * EDGE : b * side + (chunk + 1) * EDGE] = low.T
 
-    for b in range(BANDS):
-        copy_in(b).wait()
     for b in range(BANDS):
         line.add(functools.partial(own_model, b), functools.partial(weigh, b))
     line.flush()
@@ -487,11 +484,11 @@
         if step == 0:
             own_grads()
             groups.append((0, 0))
-        line.flush()
-        out_ref[step + 1] = jnp.zeros(out_ref.shape[1:], F32)
-        for group in groups:
-            collect(group)
-        done(step + 1)
+
+    line.flush()
+    out_ref[...] = jnp.zeros(out_ref.shape, F32)
+    for group in GROUPS:
+        collect(group)
 
 
 def fused_kernel(
@@ -523,7 +520,7 @@
         na, nd, place, fetched, sources, flux, position, width, tiles, params, onehot, ranks, *rest
     )
     back = GiveBack(place, partial, *to_return)
-    compute(side, sources, sky, copy_in, partial, back.start, counts, *to_compute)
+    compute(side, sources, sky, copy_in, partial, counts, *to_compute)
     back.finish(onehot, ranks, out_ref)
     for copy in sends:
         copy.wait_send()
@@ -596,11 +593,11 @@
             ],
             compute_buffers(side),
             [
-                buffer(3, near, far, LANES),
-                buffer(3, near, far, LANES),
+                buffer(near, 3, far, LANES),
+                buffer(near, 3, far, LANES),
                 buffer(far, 8, LANES),
                 buffer(far, 8, LANES),
-                dma((3, near)), dma((3, near)), dma((far,)), dma((far,)),
+                dma((near,)), dma((near,)), dma((far,)), dma((far,)),
             ],
         ],
         compiler_params=pltpu.CompilerParams(

time: 49.1 us -> 48.2 us (0.982)
  Pallas kernels: 47.4 us -> 46.2 us
    pallas_call x1, Pallas kernels: 47.4 us -> 46.2 us  [on_device(): pl.pallas_call(functools.partial(fused_kernel, na, nd, side), out_shape=j...]
where the time goes in v6:
time: 48.2 us; the launch traced here: 47.6 us
  Pallas kernels  46.2 us (96%)
  other arithmetic  1.36 us (3%)
    pallas_call x1, Pallas kernels, on_device(): pl.pallas_call(functools.partial(fused_kernel, na, nd, side), out_shape=j...  46.2 us
    reduce_sum x1, other arithmetic, on_device(): return jnp.sum(masked.reshape(RANKS, 8, rows), axis=0)  1.36 us

profile of v6, /device:TPU:1, one launch (start us, length us, event | category | flops | bytes accessed | tf_op | source)
XLA Modules:
  0.0 47.6 jit_solution(10432813259197523647)
XLA Ops:
  0.0 46.2 %fused.1 = f32[32,256]{1,0:T(8,128)} custom-call(f32[5,256]{1,0:T(8,128)} %flux_ref.1, f32[2,256]{1,0:T(2,128)} %pos_ref.1, f32[1,256]{1,0:T(1,128)} %bitcast.4, s32[1,256]{1,0:T(1,128)} %bitcast.5, f32[1,1,5]{2,1,0:T(1,128)} %sky_ref.1, s32[5,640,640]{2,1,0:T(8,128)} %counts_ref.1), custom_call_target="tpu_custom_call" | custom-call | tf_op jit(solution)/shard_map/fused/pallas_call | solution.py:568
  46.2 1.4 %bitcast_reduce_fusion = f32[8,256]{1,0:T(8,128)} fusion(f32[32,256]{1,0:T(8,128)} %fused.1), kind=kLoop, calls=%fused_computation | loop fusion | flops 6144 | bytes 40960 | tf_op jit(solution)/shard_map/reduce_sum | solution.py:608

commit v7 on v6

--- a/solution.py
+++ b/solution.py
@@ -348,6 +348,11 @@
 
     for b in range(BANDS):
         line.add(functools.partial(own_model, b), functools.partial(weigh, b))
+    most = (BANDS - 1) * side
+    begun = [
+        dot_nn(turned[:, :most], scaled[own][:most, n * 2 * LANES : (n + 1) * 2 * LANES])
+        for n in range(RANKS // 2)
+    ]
     line.flush()
 
     def fold(x):
@@ -405,10 +410,12 @@
                 lambda wide=wide: dot_nn(lhs(), rhs[:, wide]), functools.partial(consume, pair)
             )
 
-    def all_bands(group, axis, lhs, scaled_ref, prof_ref):
+    def all_bands(group, axis, lhs, scaled_ref, prof_ref, begun=None):
         base = span(group[axis])[0] + 0.5 - group[axis] * side
 
         def consume(pair, along):
+            if begun is not None:
+                along = begun[pair] + along
             for k in (2 * pair, 2 * pair + 1):
                 lanes = slice((k - 2 * pair) * LANES, (k - 2 * pair + 1) * LANES)
                 prof = prof_ref[:, k * LANES : (k + 1) * LANES]
@@ -457,7 +464,8 @@
         for start in range(0, side, EDGE):
             lhs = functools.partial(own_rows, start)
             per_band((0, 0), 0, lhs, low_j[own], prof_i[own], start, start > 0)
-        all_bands((0, 0), 1, lambda: turned[...], scaled[own], prof_j[own])
+        last = scaled[own].at[most : most + side]
+        all_bands((0, 0), 1, lambda: turned[:, most:], last, prof_j[own], begun)
 
     def collect(group):
         n, (dr, dc) = index[group], group

time: 48.2 us -> 48.2 us (level)
  no operation moved by 1% of the time
where the time goes in v7:
time: 48.2 us; the launch traced here: 47.6 us
  Pallas kernels  46.2 us (96%)
  other arithmetic  1.36 us (3%)
    pallas_call x1, Pallas kernels, on_device(): pl.pallas_call(functools.partial(fused_kernel, na, nd, side), out_shape=j...  46.2 us
    reduce_sum x1, other arithmetic, on_device(): return jnp.sum(masked.reshape(RANKS, 8, rows), axis=0)  1.36 us

profile of v7, /device:TPU:1, one launch (start us, length us, event | category | flops | bytes accessed | tf_op | source)
XLA Modules:
  0.0 47.6 jit_solution(13053381459564411535)
XLA Ops:
  0.0 46.2 %fused.1 = f32[32,256]{1,0:T(8,128)} custom-call(f32[5,256]{1,0:T(8,128)} %flux_ref.1, f32[2,256]{1,0:T(2,128)} %pos_ref.1, f32[1,256]{1,0:T(1,128)} %bitcast.4, s32[1,256]{1,0:T(1,128)} %bitcast.5, f32[1,1,5]{2,1,0:T(1,128)} %sky_ref.1, s32[5,640,640]{2,1,0:T(8,128)} %counts_ref.1), custom_call_target="tpu_custom_call" | custom-call | tf_op jit(solution)/shard_map/fused/pallas_call | solution.py:576
  46.3 1.4 %bitcast_reduce_fusion = f32[8,256]{1,0:T(8,128)} fusion(f32[32,256]{1,0:T(8,128)} %fused.1), kind=kLoop, calls=%fused_computation | loop fusion | flops 6144 | bytes 40960 | tf_op jit(solution)/shard_map/reduce_sum | solution.py:616
